TPU v7x, 128 devices: a whole 4x4x4 slice. The times are simulated.
128 devices in a mesh: ctx: 16 (over y, z), head: 8 (over x, core).
Axes of the slice: x: 4, y: 4, z: 4, core: 2. Of those that a mesh axis runs over, the one named last changes fastest.
Arguments:
- queries: bfloat16 [16384, 32, 128], P('ctx', 'head'), may hold values from -16 to 16
- keys: bfloat16 [16384, 32, 128], P('ctx', 'head'), may hold values from -16 to 16
- values: bfloat16 [16384, 32, 128], P('ctx', 'head'), may hold values from -6 to 6
- out_grad: bfloat16 [16384, 4096], P('ctx'), may hold values from -6 to 6
- wo: bfloat16 [4096, 4096], P('head', 'ctx'), may hold values from -0.125 to 0.125
Outputs:
- layer_out: bfloat16 [16384, 4096], P('ctx', 'head')
- queries_gradient: bfloat16 [16384, 32, 128], P('ctx', 'head')
- keys_gradient: bfloat16 [16384, 32, 128], P('ctx', 'head')
- values_gradient: bfloat16 [16384, 32, 128], P('ctx', 'head')
- proj_grad: bfloat16 [4096, 4096], P('head', 'ctx')
All inputs are finite; a program needn't handle non-finite values.
Results may differ from a plain program's by a relative error of at most 0.015.
Values may be sent and summed in bfloat16 or wider, within the bound.
A program may use at most 128 MiB of HBM per device.

v0:
```python
import jax
import jax.numpy as jnp
from jax import lax
from jax.sharding import PartitionSpec as P

C = 512


def attend(block_queries, block_keys, block_values, block_gradient):
    scale_factor = block_queries.shape[2] ** (-0.5)
    length = block_queries.shape[1]
    places = jnp.arange(length)
    visible = places[:, None] >= places[None, :]
    score_matrix = (
        jnp.einsum("osl,ocl->osc", block_queries, block_keys, preferred_element_type=jnp.float32)
        * scale_factor
    )
    score_matrix = jnp.where(visible[None], score_matrix, -jnp.inf)
    highest = jnp.max(score_matrix, axis=-1, keepdims=True)
    lifted = jnp.exp(score_matrix - highest)
    weights = lifted / jnp.sum(lifted, axis=-1, keepdims=True)
    rounded_scores = weights.astype(jnp.bfloat16)
    attended_values = jnp.einsum(
        "rti,ric->rtc", rounded_scores, block_values, preferred_element_type=jnp.float32
    ).astype(jnp.bfloat16)
    probability_gradient = jnp.einsum(
        "osl,ocl->osc", block_gradient, block_values, preferred_element_type=jnp.float32
    )
    score_grad = weights * (
        probability_gradient - jnp.sum(weights * probability_gradient, axis=-1, keepdims=True)
    )
    scores_lowered = score_grad.astype(jnp.bfloat16)
    queries_gradient = (
        jnp.einsum("rti,ric->rtc", scores_lowered, block_keys, preferred_element_type=jnp.float32)
        * scale_factor
    ).astype(jnp.bfloat16)
    keys_gradient = (
        jnp.einsum(
            "hfa,hfz->haz", scores_lowered, block_queries, preferred_element_type=jnp.float32
        )
        * scale_factor
    ).astype(jnp.bfloat16)
    values_gradient = jnp.einsum(
        "hfa,hfz->haz", rounded_scores, block_gradient, preferred_element_type=jnp.float32
    ).astype(jnp.bfloat16)
    return (attended_values, queries_gradient, keys_gradient, values_gradient)


def column_pass(exchanged):
    all_rows, column_count, item_count, head_dim = exchanged[0].shape

    def flatten(tensor):
        return tensor.transpose(1, 2, 0, 3).reshape(column_count * item_count, all_rows, head_dim)

    def restore(tensor):
        return tensor.reshape(column_count, item_count, all_rows, head_dim).transpose(2, 0, 1, 3)

    results = attend(
        flatten(exchanged[0]), flatten(exchanged[1]), flatten(exchanged[2]), flatten(exchanged[3])
    )
    return (
        lax.all_to_all(restore(results[0]), "ctx", split_axis=0, concat_axis=1, tiled=True),
        lax.all_to_all(restore(results[1]), "ctx", split_axis=0, concat_axis=1, tiled=True),
        lax.all_to_all(restore(results[2]), "ctx", split_axis=0, concat_axis=1, tiled=True),
        lax.all_to_all(restore(results[3]), "ctx", split_axis=0, concat_axis=1, tiled=True),
    )


def on_device(queries, keys, values, out_grad, wo):
    tokens, local_heads, head_dim = queries.shape
    row_count = tokens // C
    half = local_heads // 2
    full_weight = lax.all_gather(wo, "ctx", axis=1, tiled=True)
    attn_grad = lax.dot_general(
        out_grad, full_weight, (((1,), (1,)), ((), ())), preferred_element_type=jnp.float32
    ).astype(jnp.bfloat16)
    attn_grad = attn_grad.reshape(tokens, local_heads, head_dim)
    grids = tuple(
        (
            tensor.reshape(row_count, C, half, 2, head_dim)
            for tensor in (queries, keys, values, attn_grad)
        )
    )

    def row_layout(tensor):
        return tensor[:, :, :, 0].transpose(0, 2, 1, 3).reshape(row_count * half, C, head_dim)

    def row_restore(tensor):
        return tensor.reshape(row_count, half, C, head_dim).transpose(0, 2, 1, 3)

    strided = tuple((tensor[:, :, :, 1] for tensor in grids))
    col_parts = column_pass(
        (
            lax.all_to_all(strided[0], "ctx", split_axis=1, concat_axis=0, tiled=True),
            lax.all_to_all(strided[1], "ctx", split_axis=1, concat_axis=0, tiled=True),
            lax.all_to_all(strided[2], "ctx", split_axis=1, concat_axis=0, tiled=True),
            lax.all_to_all(strided[3], "ctx", split_axis=1, concat_axis=0, tiled=True),
        )
    )
    row_results = attend(
        row_layout(grids[0]), row_layout(grids[1]), row_layout(grids[2]), row_layout(grids[3])
    )
    row_parts = tuple((row_restore(tensor) for tensor in row_results))
    joined = tuple(
        (
            jnp.stack([row_parts[index], col_parts[index]], axis=3).reshape(
                tokens, local_heads, head_dim
            )
            for index in range(4)
        )
    )
    flat_attn = joined[0].reshape(tokens, local_heads * head_dim)
    partial_out = jnp.dot(flat_attn, full_weight, preferred_element_type=jnp.float32)
    layer_out = lax.psum_scatter(
        partial_out.astype(jnp.bfloat16), "head", scatter_dimension=1, tiled=True
    )
    grad_term = lax.dot_general(
        flat_attn, out_grad, (((0,), (0,)), ((), ())), preferred_element_type=jnp.float32
    )
    proj_grad = lax.psum_scatter(
        grad_term.astype(jnp.bfloat16), "ctx", scatter_dimension=1, tiled=True
    )
    return (layer_out, joined[1], joined[2], joined[3], proj_grad)


def solution(mesh):
    in_specs = (
        P("ctx", "head", None),
        P("ctx", "head", None),
        P("ctx", "head", None),
        P("ctx", None),
        P("head", "ctx"),
    )
    out_specs = (
        P("ctx", "head"),
        P("ctx", "head", None),
        P("ctx", "head", None),
        P("ctx", "head", None),
        P("head", "ctx"),
    )
    return jax.shard_map(
        on_device, mesh=mesh, in_specs=in_specs, out_specs=out_specs, check_vma=False
    )
```

profile of v0, /device:TPU:1, one launch (start us, length us, event | category | flops | bytes accessed | tf_op | source)
XLA Modules:
  0.0 241.7 jit_solution(15036941549528151766)
XLA Ops:
  10.7 8.6 %all-to-all-start = ((bf16[2,512,2,128]{3,2,0,1:T(2,128)(2,1)}), bf16[2,512,2,128]{3,2,0,1:T(2,128)(2,1)S(1)}, u32[]{:S(2)}, u32[]{:S(2)}) async-start(bf16[2,512,2,128]{3,2,0,1:T(2,128)(2,1)} %copy.111), calls=%async_computation | async-start | bytes 1048576 | tf_op jit(solution)/shard_map/all_to_all | solution.py:94
  20.8 8.7 %all-to-all-done = bf16[2,512,2,128]{3,2,0,1:T(2,128)(2,1)S(1)} async-done(((bf16[2,512,2,128]{3,2,0,1:T(2,128)(2,1)}), bf16[2,512,2,128]{3,2,0,1:T(2,128)(2,1)S(1)}, u32[]{:S(2)}, u32[]{:S(2)}) %all-to-all-start) | async-done | bytes 524320 | tf_op jit(solution)/shard_map/all_to_all | solution.py:94
  29.6 3.6 %all-to-all-start.1 = ((bf16[2,512,2,128]{3,2,0,1:T(2,128)(2,1)}), bf16[2,512,2,128]{3,2,0,1:T(2,128)(2,1)S(1)}, u32[]{:S(2)}, u32[]{:S(2)}) async-start(bf16[2,512,2,128]{3,2,0,1:T(2,128)(2,1)} %copy.114), calls=%async_computation.1 | async-start | bytes 1048576 | tf_op jit(solution)/shard_map/all_to_all | solution.py:95
  36.0 6.2 %all-to-all-done.1 = bf16[2,512,2,128]{3,2,0,1:T(2,128)(2,1)S(1)} async-done(((bf16[2,512,2,128]{3,2,0,1:T(2,128)(2,1)}), bf16[2,512,2,128]{3,2,0,1:T(2,128)(2,1)S(1)}, u32[]{:S(2)}, u32[]{:S(2)}) %all-to-all-start.1) | async-done | bytes 524320 | tf_op jit(solution)/shard_map/all_to_all | solution.py:95
  42.2 4.1 %all-to-all-start.2 = ((bf16[2,512,2,128]{3,2,0,1:T(2,128)(2,1)}), bf16[2,512,2,128]{3,2,0,1:T(2,128)(2,1)S(1)}, u32[]{:S(2)}, u32[]{:S(2)}) async-start(bf16[2,512,2,128]{3,2,0,1:T(2,128)(2,1)} %copy.117), calls=%async_computation.2 | async-start | bytes 1048576 | tf_op jit(solution)/shard_map/all_to_all | solution.py:96
  48.2 4.6 %fusion.23 = (f32[4,512]{1,0:T(4,128)S(1)}, f32[4,512,512]{1,2,0:T(8,128)}) fusion(pred[512,512]{0,1:T(8,128)(4,1)S(1)} %iota_compare_fusion, bf16[4,512,128]{2,1,0:T(8,128)(2,1)} %bitcast.181, bf16[4,512,128]{2,1,0:T(8,128)(2,1)S(1)} %bitcast.169), kind=kOutput, calls=%fused_computation.59 | convolution fusion | flops 272630272 | bytes 5513216 | tf_op jit(solution)/shard_map/sub | solution.py:20
  60.7 5.3 %all-to-all-start.3 = ((bf16[32,32,2,128]{3,1,2,0:T(8,128)(2,1)}), bf16[32,32,2,128]{3,1,2,0:T(8,128)(2,1)S(1)}, u32[]{:S(2)}, u32[]{:S(2)}) async-start(bf16[32,32,2,128]{3,1,2,0:T(8,128)(2,1)} %bitcast.151), calls=%async_computation.3 | async-start | bytes 1048576 | tf_op jit(solution)/shard_map/all_to_all | solution.py:62
  66.2 3.1 %convolution_convert_fusion.6 = bf16[4,512,128]{2,1,0:T(8,128)(2,1)S(1)} fusion(bf16[4,512,128]{2,1,0:T(8,128)(2,1)S(1)} %bitcast.185, f32[4,512,512]{1,2,0:T(8,128)} %get-tuple-element.16, f32[4,512]{1,0:T(4,128)S(1)} %get-tuple-element.15), kind=kOutput, calls=%fused_computation.25 | convolution fusion | flops 270794752 | bytes 5251072 | tf_op jit(solution)/shard_map/rti,ric->rtc/dot_general | solution.py:23
  69.3 6.3 %all-to-all-done.3 = bf16[32,32,2,128]{3,1,2,0:T(8,128)(2,1)S(1)} async-done(((bf16[32,32,2,128]{3,1,2,0:T(8,128)(2,1)}), bf16[32,32,2,128]{3,1,2,0:T(8,128)(2,1)S(1)}, u32[]{:S(2)}, u32[]{:S(2)}) %all-to-all-start.3) | async-done | bytes 524320 | tf_op jit(solution)/shard_map/all_to_all | solution.py:62
  77.3 9.5 %convolution_convert_fusion.1 = bf16[512,4096]{1,0:T(8,128)(2,1)} fusion(bf16[1024,512]{1,0:T(8,128)(2,1)S(1)} %reshape_reshape.6, bf16[1024,4096]{1,0:T(8,128)(2,1)} %param.8), kind=kOutput, calls=%fused_computation.3 | convolution fusion | flops 4297064448 | bytes 13631488 | tf_op jit(solution)/shard_map/dot_general | solution.py:117
  87.0 8.9 %convolution_convert_fusion = bf16[1024,4096]{1,0:T(8,128)(2,1)} fusion(bf16[1024,512]{1,0:T(8,128)(2,1)S(1)} %reshape_reshape.6, bf16[512,4096]{1,0:T(8,128)(2,1)} %all-gather.2.cloned.1.call-done), kind=kOutput, calls=%fused_computation.2 | convolution fusion | flops 4299161600 | bytes 13631488 | tf_op jit(solution)/shard_map/dot_general | solution.py:113
  95.9 9.1 %convolution_convert_fusion.2 = bf16[1024,512]{1,0:T(8,128)(2,1)S(1)} fusion(bf16[1024,4096]{1,0:T(8,128)(2,1)} %param.8, bf16[512,4096]{1,0:T(8,128)(2,1)} %all-gather.2.cloned.1.call-done), kind=kOutput, calls=%fused_computation.13 | convolution fusion | flops 4295491584 | bytes 13631488 | tf_op jit(solution)/shard_map/dot_general | solution.py:74
  108.3 3.7 %all-to-all-start.4 = ((bf16[2,512,2,128]{3,2,0,1:T(2,128)(2,1)}), bf16[2,512,2,128]{3,2,0,1:T(2,128)(2,1)S(1)}, u32[]{:S(2)}, u32[]{:S(2)}) async-start(bf16[2,512,2,128]{3,2,0,1:T(2,128)(2,1)} %copy.127), calls=%async_computation.5 | async-start | bytes 1048576 | tf_op jit(solution)/shard_map/all_to_all | solution.py:97
  112.1 3.2 %multiply_reduce_fusion = (f32[4,512]{1,0:T(4,128)S(1)}, f32[4,512,512]{1,2,0:T(8,128)S(1)}) fusion(f32[4,512,512]{1,2,0:T(8,128)} %get-tuple-element.16, f32[4,512]{1,0:T(4,128)S(1)} %get-tuple-element.15, bf16[4,512,128]{2,1,0:T(8,128)(2,1)S(1)} %bitcast.179, bf16[4,512,128]{2,1,0:T(8,128)(2,1)S(1)} %bitcast.186), kind=kOutput, calls=%fused_computation.5 | convolution fusion | flops 271579136 | bytes 9453568 | tf_op jit(solution)/shard_map/osl,ocl->osc/dot_general | solution.py:26
  118.6 4.0 %all-to-all-done.4 = bf16[2,512,2,128]{3,2,0,1:T(2,128)(2,1)S(1)} async-done(((bf16[2,512,2,128]{3,2,0,1:T(2,128)(2,1)}), bf16[2,512,2,128]{3,2,0,1:T(2,128)(2,1)S(1)}, u32[]{:S(2)}, u32[]{:S(2)}) %all-to-all-start.4) | async-done | bytes 524320 | tf_op jit(solution)/shard_map/all_to_all | solution.py:97
  123.8 3.1 %convolution_convert_fusion.3 = bf16[64,32,128]{2,1,0:T(8,128)(2,1)} fusion(bf16[64,32,128]{2,1,0:T(8,128)(2,1)} %bitcast.187, f32[64,32]{1,0:T(8,128)S(1)} %get-tuple-element.13, f32[64,32,32]{1,2,0:T(8,128)} %copy-done.3), kind=kOutput, calls=%fused_computation.22 | convolution fusion | flops 17238048 | bytes 1318912 | tf_op jit(solution)/shard_map/hfa,hfz->haz/dot_general | solution.py:43
  129.3 4.5 %all-to-all-start.7 = ((bf16[32,32,2,128]{3,2,1,0:T(2,128)(2,1)}), bf16[32,32,2,128]{3,2,1,0:T(2,128)(2,1)}, u32[]{:S(2)}, u32[]{:S(2)}) async-start(bf16[32,32,2,128]{3,2,1,0:T(2,128)(2,1)} %bitcast.148), calls=%async_computation.8 | async-start | bytes 1048576 | tf_op jit(solution)/shard_map/all_to_all | solution.py:65
  137.8 5.5 %all-to-all-done.7 = bf16[32,32,2,128]{3,2,1,0:T(2,128)(2,1)} async-done(((bf16[32,32,2,128]{3,2,1,0:T(2,128)(2,1)}), bf16[32,32,2,128]{3,2,1,0:T(2,128)(2,1)}, u32[]{:S(2)}, u32[]{:S(2)}) %all-to-all-start.7) | async-done | bytes 524320 | tf_op jit(solution)/shard_map/all_to_all | solution.py:65
  143.3 4.3 %all-to-all-start.6 = ((bf16[32,32,2,128]{3,2,1,0:T(2,128)(2,1)}), bf16[32,32,2,128]{3,2,1,0:T(2,128)(2,1)}, u32[]{:S(2)}, u32[]{:S(2)}) async-start(bf16[32,32,2,128]{3,2,1,0:T(2,128)(2,1)} %bitcast.166), calls=%async_computation.7 | async-start | bytes 1048576 | tf_op jit(solution)/shard_map/all_to_all | solution.py:64
  152.0 5.0 %all-to-all-done.6 = bf16[32,32,2,128]{3,2,1,0:T(2,128)(2,1)} async-done(((bf16[32,32,2,128]{3,2,1,0:T(2,128)(2,1)}), bf16[32,32,2,128]{3,2,1,0:T(2,128)(2,1)}, u32[]{:S(2)}, u32[]{:S(2)}) %all-to-all-start.6) | async-done | bytes 524320 | tf_op jit(solution)/shard_map/all_to_all | solution.py:64
  157.0 3.6 %all-to-all-start.5 = ((bf16[32,32,2,128]{3,2,1,0:T(2,128)(2,1)}), bf16[32,32,2,128]{3,2,1,0:T(2,128)(2,1)S(1)}, u32[]{:S(2)}, u32[]{:S(2)}) async-start(bf16[32,32,2,128]{3,2,1,0:T(2,128)(2,1)} %bitcast.150), calls=%async_computation.6 | async-start | bytes 1048576 | tf_op jit(solution)/shard_map/all_to_all | solution.py:63
  160.6 3.0 %convolution_convert_fusion.5 = bf16[4,512,128]{2,1,0:T(8,128)(2,1)S(1)} fusion(bf16[4,512,128]{2,1,0:T(8,128)(2,1)} %bitcast.180, f32[4,512,512]{1,2,0:T(8,128)} %get-tuple-element.16, f32[4,512]{1,0:T(4,128)S(1)} %get-tuple-element.15), kind=kOutput, calls=%fused_computation.24 | convolution fusion | flops 270794752 | bytes 5251072 | tf_op jit(solution)/shard_map/hfa,hfz->haz/dot_general | solution.py:43
  165.9 4.3 %all-to-all-done.5 = bf16[32,32,2,128]{3,2,1,0:T(2,128)(2,1)S(1)} async-done(((bf16[32,32,2,128]{3,2,1,0:T(2,128)(2,1)}), bf16[32,32,2,128]{3,2,1,0:T(2,128)(2,1)S(1)}, u32[]{:S(2)}, u32[]{:S(2)}) %all-to-all-start.5) | async-done | bytes 524320 | tf_op jit(solution)/shard_map/all_to_all | solution.py:63
  179.3 55.8 %reduce-scatter.3.cloned.1.call-done = bf16[1024,512]{1,0:T(8,128)(2,1)} async-done(((bf16[1024,4096]{1,0:T(8,128)(2,1)}), bf16[1024,512]{1,0:T(8,128)(2,1)}) %reduce-scatter.3.cloned.1.call-update) | async-done | bytes 1048592 | tf_op jit(solution)/shard_map/reduce_scatter | solution.py:114
  (89 shorter events, 49.5 us)
Async XLA Ops:
  7.2 12.1 %copy-start.7 = (bf16[1024,4,128]{2,1,0:T(4,128)(2,1)S(1)}, bf16[1024,4,128]{2,1,0:T(4,128)(2,1)}, u32[]{:S(2)}) copy-start(bf16[1024,4,128]{2,1,0:T(4,128)(2,1)} %param.6) | copy-start | bytes 3145732
  7.2 79.8 %all-gather.2.cloned.1.call-start = ((), (), s32[]{:S(2)}) async-start(), calls=%async_computation.10 | async-start | bytes 4456448 | tf_op jit(solution)/shard_map/all_gather | solution.py:73
  10.7 18.9 %all-to-all-start = ((bf16[2,512,2,128]{3,2,0,1:T(2,128)(2,1)}), bf16[2,512,2,128]{3,2,0,1:T(2,128)(2,1)S(1)}, u32[]{:S(2)}, u32[]{:S(2)}) async-start(bf16[2,512,2,128]{3,2,0,1:T(2,128)(2,1)} %copy.111), calls=%async_computation | async-start | bytes 1048576 | tf_op jit(solution)/shard_map/all_to_all | solution.py:94
  29.6 12.6 %all-to-all-start.1 = ((bf16[2,512,2,128]{3,2,0,1:T(2,128)(2,1)}), bf16[2,512,2,128]{3,2,0,1:T(2,128)(2,1)S(1)}, u32[]{:S(2)}, u32[]{:S(2)}) async-start(bf16[2,512,2,128]{3,2,0,1:T(2,128)(2,1)} %copy.114), calls=%async_computation.1 | async-start | bytes 1048576 | tf_op jit(solution)/shard_map/all_to_all | solution.py:95
  42.2 13.0 %all-to-all-start.2 = ((bf16[2,512,2,128]{3,2,0,1:T(2,128)(2,1)}), bf16[2,512,2,128]{3,2,0,1:T(2,128)(2,1)S(1)}, u32[]{:S(2)}, u32[]{:S(2)}) async-start(bf16[2,512,2,128]{3,2,0,1:T(2,128)(2,1)} %copy.117), calls=%async_computation.2 | async-start | bytes 1048576 | tf_op jit(solution)/shard_map/all_to_all | solution.py:96
  47.2 5.6 %copy-start.5 = (bf16[2,2,512,128]{3,2,1,0:T(8,128)(2,1)}, bf16[2,2,512,128]{3,2,1,0:T(8,128)(2,1)S(1)}, u32[]{:S(2)}) copy-start(bf16[2,2,512,128]{3,2,1,0:T(8,128)(2,1)S(1)} %copy.106) | copy-start | bytes 1572868
  53.3 5.3 %copy-start = (bf16[16,2,32,2,128]{4,1,0,3,2:T(2,128)(2,1)}, bf16[16,2,32,2,128]{4,1,0,3,2:T(2,128)(2,1)S(1)}, u32[]{:S(2)}) copy-start(bf16[16,2,32,2,128]{4,1,0,3,2:T(2,128)(2,1)S(1)} %copy.112) | copy-start | bytes 1572868
  55.6 2.9 %copy-start.10 = (bf16[16,2,32,2,128]{4,1,0,3,2:T(2,128)(2,1)}, bf16[16,2,32,2,128]{4,1,0,3,2:T(2,128)(2,1)S(1)}, u32[]{:S(2)}) copy-start(bf16[16,2,32,2,128]{4,1,0,3,2:T(2,128)(2,1)S(1)} %copy.118) | copy-start | bytes 1572868
  56.0 4.7 %copy-start.3 = (f32[64,32,32]{1,2,0:T(8,128)}, f32[64,32,32]{1,2,0:T(8,128)S(1)}, u32[]{:S(2)}) copy-start(f32[64,32,32]{1,2,0:T(8,128)S(1)} %fusion.8) | copy-start | bytes 786436
  56.0 10.2 %copy-start.12 = (bf16[2,2,512,128]{3,2,1,0:T(8,128)(2,1)S(1)}, bf16[2,2,512,128]{3,2,1,0:T(8,128)(2,1)}, u32[]{:S(2)}) copy-start(bf16[2,2,512,128]{3,2,1,0:T(8,128)(2,1)} %copy.108) | copy-start | bytes 1572868
  60.7 14.9 %all-to-all-start.3 = ((bf16[32,32,2,128]{3,1,2,0:T(8,128)(2,1)}), bf16[32,32,2,128]{3,1,2,0:T(8,128)(2,1)S(1)}, u32[]{:S(2)}, u32[]{:S(2)}) async-start(bf16[32,32,2,128]{3,1,2,0:T(8,128)(2,1)} %bitcast.151), calls=%async_computation.3 | async-start | bytes 1048576 | tf_op jit(solution)/shard_map/all_to_all | solution.py:62
  66.0 113.3 %reduce-scatter.5.cloned.1.call-start = ((), (), s32[]{:S(2)}) async-start(), calls=%async_computation.12 | async-start | bytes 4456448 | tf_op jit(solution)/shard_map/reduce_scatter | solution.py:120
  86.9 148.3 %reduce-scatter.3.cloned.1.call-start = ((), (), s32[]{:S(2)}) async-start(), calls=%async_computation.11 | async-start | bytes 9437184 | tf_op jit(solution)/shard_map/reduce_scatter | solution.py:114
  105.3 6.8 %copy-start.13 = (bf16[2,2,512,128]{3,2,1,0:T(8,128)(2,1)S(1)}, bf16[2,2,512,128]{3,2,1,0:T(8,128)(2,1)}, u32[]{:S(2)}) copy-start(bf16[2,2,512,128]{3,2,1,0:T(8,128)(2,1)} %copy.108) | copy-start | bytes 1572868
  106.9 8.4 %copy-start.8 = (bf16[2,512,2,1,128]{4,1,3,2,0:T(8,128)(2,1)}, bf16[2,512,2,1,128]{4,1,3,2,0:T(8,128)(2,1)S(1)}, u32[]{:S(2)}) copy-start(bf16[2,512,2,1,128]{4,1,3,2,0:T(8,128)(2,1)S(1)} %copy.149) | copy-start | bytes 1572868
  108.3 14.2 %all-to-all-start.4 = ((bf16[2,512,2,128]{3,2,0,1:T(2,128)(2,1)}), bf16[2,512,2,128]{3,2,0,1:T(2,128)(2,1)S(1)}, u32[]{:S(2)}, u32[]{:S(2)}) async-start(bf16[2,512,2,128]{3,2,0,1:T(2,128)(2,1)} %copy.127), calls=%async_computation.5 | async-start | bytes 1048576 | tf_op jit(solution)/shard_map/all_to_all | solution.py:97
  112.1 3.7 %copy-start.2 = (f32[4,512,512]{1,2,0:T(8,128)S(1)}, f32[4,512,512]{1,2,0:T(8,128)}, u32[]{:S(2)}) copy-start(f32[4,512,512]{1,2,0:T(8,128)} %get-tuple-element.16) | copy-start | bytes 12582916
  123.8 10.0 %copy-start.11 = (bf16[16,2,32,2,128]{4,1,0,3,2:T(2,128)(2,1)S(1)}, bf16[16,2,32,2,128]{4,1,0,3,2:T(2,128)(2,1)}, u32[]{:S(2)}) copy-start(bf16[16,2,32,2,128]{4,1,0,3,2:T(2,128)(2,1)} %copy-done.10) | copy-start | bytes 1572868
  129.3 14.0 %all-to-all-start.7 = ((bf16[32,32,2,128]{3,2,1,0:T(2,128)(2,1)}), bf16[32,32,2,128]{3,2,1,0:T(2,128)(2,1)}, u32[]{:S(2)}, u32[]{:S(2)}) async-start(bf16[32,32,2,128]{3,2,1,0:T(2,128)(2,1)} %bitcast.148), calls=%async_computation.8 | async-start | bytes 1048576 | tf_op jit(solution)/shard_map/all_to_all | solution.py:65
  133.8 2.3 copy-start.1
  143.3 13.7 %all-to-all-start.6 = ((bf16[32,32,2,128]{3,2,1,0:T(2,128)(2,1)}), bf16[32,32,2,128]{3,2,1,0:T(2,128)(2,1)}, u32[]{:S(2)}, u32[]{:S(2)}) async-start(bf16[32,32,2,128]{3,2,1,0:T(2,128)(2,1)} %bitcast.166), calls=%async_computation.7 | async-start | bytes 1048576 | tf_op jit(solution)/shard_map/all_to_all | solution.py:64
  157.0 13.2 %all-to-all-start.5 = ((bf16[32,32,2,128]{3,2,1,0:T(2,128)(2,1)}), bf16[32,32,2,128]{3,2,1,0:T(2,128)(2,1)S(1)}, u32[]{:S(2)}, u32[]{:S(2)}) async-start(bf16[32,32,2,128]{3,2,1,0:T(2,128)(2,1)} %bitcast.150), calls=%async_computation.6 | async-start | bytes 1048576 | tf_op jit(solution)/shard_map/all_to_all | solution.py:63
  163.6 8.9 %copy-start.6 = (bf16[4,512,128]{2,1,0:T(8,128)(2,1)S(1)}, bf16[4,512,128]{2,1,0:T(8,128)(2,1)}, u32[]{:S(2)}) copy-start(bf16[4,512,128]{2,1,0:T(8,128)(2,1)} %fusion.9) | copy-start | bytes 1572868
  170.3 4.3 %copy-start.14 = (bf16[4,512,128]{2,1,0:T(8,128)(2,1)S(1)}, bf16[4,512,128]{2,1,0:T(8,128)(2,1)}, u32[]{:S(2)}) copy-start(bf16[4,512,128]{2,1,0:T(8,128)(2,1)} %fusion.10) | copy-start | bytes 1572868
  (2 other events, 3.2 us)
Sparse Core Ops, SparseCore 0:
  10.1 69.0 all-gather.1
  87.0 92.2 reduce-scatter.4
  182.3 52.8 reduce-scatter.2
where the time goes:
time: 243 us; the launch traced here: 242 us
  waiting for transfers between devices  101 us (42%)
  matrix products  53 us (22%)
  starting transfers between devices  37.9 us (16%)
  local copies, waits for them, and re-layouts  32.8 us (13%)
  between operations  14.2 us (6%)
  other arithmetic  3.21 us (1%)
    reduce_scatter x1, waiting for transfers between devices, on_device(): lax.psum_scatter(partial_out.astype(jnp.bfloat16), 'head', scatter_dimens...  55.8 us
    dot_general x1, matrix products, on_device(): lax.dot_general(flat_attn, out_grad, (((0,), (0,)), ((), ())), preferred_...  9.52 us
    dot_general x1, matrix products, on_device(): lax.dot_general(out_grad, full_weight, (((1,), (1,)), ((), ())), preferre...  9.09 us
    dot_general x1, matrix products, on_device(): jnp.dot(flat_attn, full_weight, preferred_element_type=jnp.float32)  8.91 us
    all_to_all x1, waiting for transfers between devices, on_device(): lax.all_to_all(strided[0], 'ctx', split_axis=1, concat_axis=0, tiled=True)  8.75 us
    all_to_all x1, starting transfers between devices, on_device(): lax.all_to_all(strided[0], 'ctx', split_axis=1, concat_axis=0, tiled=True)  8.59 us
    reshape x4, local copies, waits for them, and re-layouts, restore(): tensor.reshape(column_count, item_count, all_rows, head_dim)  7.24 us
    another operation x4, local copies, waits for them, and re-layouts, on_device(): jnp.stack([row_parts[index], col_parts[index]], axis=3)  7.23 us
  transfers between devices with their start and end apart: 11, of which 10 were waited for; matrix products, arithmetic and copies ran while one was open for 37% of the time, Pallas kernels for 0%

commit v1 on v0

v1 whole, which is shorter than its diff:
```python
import jax
import jax.numpy as jnp
from jax import lax
from jax.experimental import pallas as pl
from jax.experimental.pallas import tpu as pltpu
from jax.sharding import PartitionSpec as P

MESH = pl.DeviceIdType.MESH
BF16 = jnp.bfloat16
F32 = jnp.float32
SCALE = 128 ** -0.5
SEVEN = tuple((dy, dz) for dy in range(4) for dz in range(4) if dy or dz)


def nt(a, b):
    return lax.dot_general(a, b, (((1,), (1,)), ((), ())), preferred_element_type=F32)


def nn(a, b):
    return lax.dot_general(a, b, (((1,), (0,)), ((), ())), preferred_element_type=F32)


def tn(a, b):
    return lax.dot_general(a, b, (((0,), (0,)), ((), ())), preferred_element_type=F32)


def softmax(scores, visible):
    scores = jnp.where(visible, scores * SCALE, -jnp.inf)
    lifted = jnp.exp(scores - jnp.max(scores, axis=-1, keepdims=True))
    return lifted / jnp.sum(lifted, axis=-1, keepdims=True)


def score_gradient(p, dp):
    return (p * (dp - jnp.sum(p * dp, axis=-1, keepdims=True))).astype(BF16)


def kernel(
    qr, kr, vr, qs, ks, vs, og_hbm, wo_hbm,
    lay_out, dqr, dkr, dvr, dqs, dks, dvs, pg_out,
    W, OG, QKVR, REC, RDO, SO, RO, SDO, SG, PC, PR, ATT, ATTT, AGF, AGR, PP, R1, S2, R2, LS, LR, LX, DR, PG,
    loc, qkv_s, qkv_r, o_s, o_r, do_s, do_r, dg_s, dg_r, w1_s, w1_r, wa_s, wa_r, wb_s, wb_r,
    p1_s, p1_r, p2_s, p2_r, lp_s, lp_r, lx_s, lx_r,
):
    c = lax.axis_index("ctx")
    h = lax.axis_index("head")
    y, z = c // 4, lax.rem(c, 4)
    x, core = h // 2, lax.rem(h, 2)

    def grid_peer(dy, dz):
        return lax.rem(y + dy, 4) * 4 + lax.rem(z + dz, 4)

    def x_head(dx):
        return lax.rem(x + dx, 4) * 2 + core

    partner = (c, x * 2 + (1 - core))

    def remote(src, dst, ssem, rsem, dev):
        return pltpu.make_async_remote_copy(
            src_ref=src, dst_ref=dst, send_sem=ssem, recv_sem=rsem, device_id=dev, device_id_type=MESH
        )

    sends = []

    def push(copy):
        copy.start()
        sends.append(copy)
        return copy

    own_cols = pl.ds(pl.multiple_of(c * 256, 256), 256)

    loads_w = []
    for slot, j in enumerate((0, 2, 1, 3)):
        copy = pltpu.make_async_copy(
            wo_hbm.at[pl.ds(j * 128, 128)], W.at[pl.ds(slot * 128, 128), own_cols], loc.at[slot]
        )
        copy.start()
        loads_w.append(copy)
    loads_r = []
    for t, src in enumerate((qr, kr, vr)):
        copy = pltpu.make_async_copy(src, QKVR.at[t], loc.at[4 + t])
        copy.start()
        loads_r.append(copy)
    loads_s = []
    for t, src in enumerate((qs, ks, vs)):
        copy = pltpu.make_async_copy(src.at[c], REC.at[t, c], loc.at[7 + t])
        copy.start()
        loads_s.append(copy)
    load_og = pltpu.make_async_copy(og_hbm, OG, loc.at[10])
    load_og.start()

    barrier = pltpu.get_barrier_semaphore()
    for dy, dz in SEVEN:
        pl.semaphore_signal(barrier, inc=1, device_id=(grid_peer(dy, dz), h), device_id_type=MESH)
    for dx in range(1, 4):
        pl.semaphore_signal(barrier, inc=1, device_id=(c, x_head(dx)), device_id_type=MESH)
    pl.semaphore_signal(barrier, inc=1, device_id=partner, device_id_type=MESH)
    pl.semaphore_wait(barrier, 19)

    qkv_in = []
    for t, src in enumerate((qs, ks, vs)):
        for i, (dy, dz) in enumerate(SEVEN):
            to = grid_peer(dy, dz)
            qkv_in.append(push(remote(src.at[to], REC.at[t, c], qkv_s.at[t, i], qkv_r.at[t, i], (to, h))))

    for copy in loads_w:
        copy.wait()
    w_own = W.at[:, own_cols]
    wz, wy = [], []
    for d in range(1, 4):
        wz.append(push(remote(w_own, w_own, w1_s.at[d - 1], w1_r.at[d - 1], (grid_peer(0, d), h))))
        wy.append(push(remote(w_own, w_own, w1_s.at[2 + d], w1_r.at[2 + d], (grid_peer(d, 0), h))))

    for copy in loads_r:
        copy.wait()

    def causal(rows, cols, first):
        return (
            lax.broadcasted_iota(jnp.int32, (rows, cols), 0) + first
            >= lax.broadcasted_iota(jnp.int32, (rows, cols), 1)
        )

    def row_forward(i, carry):
        r, hh = i // 2, lax.rem(i, 2)
        lanes = pl.ds(pl.multiple_of(hh * 128, 128), 128)
        for b in range(2):
            n = 256 * (b + 1)
            q = QKVR[0, i, pl.ds(256 * b, 256), :]
            p = softmax(nt(q, QKVR[1, i, pl.ds(0, n), :]), causal(256, n, 256 * b))
            PR[i, pl.ds(256 * b, 256), pl.ds(0, n)] = p
            o = nn(p.astype(BF16), QKVR[2, i, pl.ds(0, n), :])
            rows = pl.ds(pl.multiple_of(r * 512 + 256 * b, 256), 256)
            ATT[rows, lanes] = o.astype(BF16)
            ATTT[lanes, rows] = o.T.astype(BF16)
        return carry

    lax.fori_loop(0, 4, row_forward, 0)

    def projection(half):
        def one(n, carry):
            cols = pl.ds(pl.multiple_of(n * 256, 256), 256)
            part = nn(ATTT[pl.ds(256 * half, 256), :], OG[:, cols])
            PP[half, n // 4, lax.rem(n, 4)] = part.astype(BF16)
            return carry

        lax.fori_loop(0, 16, one, 0)

    load_og.wait()
    projection(0)

    for copy in qkv_in:
        copy.wait_recv()
    for copy in loads_s:
        copy.wait()
    ii = lax.broadcasted_iota(jnp.int32, (256, 256), 0)
    jj = lax.broadcasted_iota(jnp.int32, (256, 256), 1)

    def tile(ref):
        return ref.reshape(256, 128)

    def col_forward(i, carry):
        hh, g = i // 4, lax.rem(i, 4)
        visible = (lax.rem(ii, 8) == lax.rem(jj, 8)) & (ii >= jj)
        p = softmax(nt(tile(REC[0, :, hh, g]), tile(REC[1, :, hh, g])), visible)
        PC[i] = p
        o = nn(p.astype(BF16), tile(REC[2, :, hh, g]))
        SO[:, hh, g] = o.astype(BF16).reshape(16, 16, 128)
        return carry

    lax.fori_loop(0, 8, col_forward, 0)
    o_in = []
    for i, (dy, dz) in enumerate(SEVEN):
        to = grid_peer(dy, dz)
        o_in.append(push(remote(SO.at[to], RO.at[c], o_s.at[i], o_r.at[i], (to, h))))
    RO[c] = SO[c]

    wa, wb = [], []
    for d in range(1, 4):
        wz[d - 1].wait_recv()
        block = W.at[pl.ds(0, 256), pl.ds(pl.multiple_of(grid_peer(0, 4 - d) * 256, 256), 256)]
        for e in range(1, 4):
            k = 3 * (d - 1) + e - 1
            wa.append(push(remote(block, block, wa_s.at[k], wa_r.at[k], (grid_peer(e, 0), h))))
        wy[d - 1].wait_recv()
        block = W.at[pl.ds(256, 256), pl.ds(pl.multiple_of(grid_peer(4 - d, 0) * 256, 256), 256)]
        for e in range(1, 4):
            k = 3 * (d - 1) + e - 1
            wb.append(push(remote(block, block, wb_s.at[k], wb_r.at[k], (grid_peer(0, e), h))))

    for copy in o_in:
        copy.wait_recv()
    for hh in range(2):
        for g in range(4):
            block = RO[:, hh, g].astype(F32)
            for r in range(2):
                AGF[r, :, g, :, pl.ds(hh * 128, 128)] = block[:, 8 * r : 8 * r + 8, :]

    def place(m, carry):
        block = AGF[m // 2, pl.ds(pl.multiple_of(lax.rem(m, 2) * 8, 8), 8)].reshape(256, 256)
        rows = pl.ds(pl.multiple_of(m * 256, 256), 256)
        ATT[rows, pl.ds(256, 256)] = block.astype(BF16)
        ATTT[pl.ds(256, 256), rows] = block.T.astype(BF16)
        return carry

    lax.fori_loop(0, 4, place, 0)
    projection(1)

    for copy in wb:
        copy.wait_recv()
    for copy in wa:
        copy.wait_recv()

    def strided_cotangent(m, carry):
        rows = pl.ds(pl.multiple_of(m * 256, 256), 256)
        part = nt(OG[rows, :], W[pl.ds(256, 256), :])
        AGF[m // 2, pl.ds(pl.multiple_of(lax.rem(m, 2) * 8, 8), 8)] = part.reshape(8, 4, 8, 256)
        return carry

    lax.fori_loop(0, 4, strided_cotangent, 0)
    for hh in range(2):
        for g in range(4):
            lanes = pl.ds(hh * 128, 128)
            both = jnp.concatenate([AGF[0, :, g, :, lanes], AGF[1, :, g, :, lanes]], axis=1)
            SDO[:, hh, g] = both.astype(BF16)
    do_in = []
    for i, (dy, dz) in enumerate(SEVEN):
        to = grid_peer(dy, dz)
        do_in.append(push(remote(SDO.at[to], RDO.at[c], do_s.at[i], do_r.at[i], (to, h))))
    RDO[c] = SDO[c]

    p1_in = []
    for d in range(1, 4):
        to = lax.rem(z + d, 4)
        p1_in.append(
            push(remote(PP.at[0, :, to], R1.at[0, d - 1], p1_s.at[0, d - 1], p1_r.at[0, d - 1], (grid_peer(0, d), h)))
        )
        to = lax.rem(y + d, 4)
        p1_in.append(
            push(remote(PP.at[1, to], R1.at[1, d - 1], p1_s.at[1, d - 1], p1_r.at[1, d - 1], (grid_peer(d, 0), h)))
        )

    def partial_out(m, head):
        rows = pl.ds(pl.multiple_of(m * 256, 256), 256)
        cols = pl.ds(pl.multiple_of(head * 512, 512), 512)
        return rows, nn(ATT[rows, :], W[:, cols])

    lp_in = []
    for n, dx in enumerate((2, 1, 3, 0)):
        head = lax.rem(x + dx, 4) * 2 + (1 - core)

        def for_partner(m, carry, n=n, head=head):
            rows, part = partial_out(m, head)
            LS[n, rows, :] = part.astype(BF16)
            return carry

        lax.fori_loop(0, 4, for_partner, 0)
        lp_in.append(push(remote(LS.at[n], LR.at[n], lp_s.at[n], lp_r.at[n], partner)))

    lx_in = []
    for n, dx in enumerate((2, 1, 3, 0)):
        head = x_head(dx)
        lp_in[n].wait_recv()

        def for_x(m, carry, n=n, head=head):
            rows, part = partial_out(m, head)
            LR[n, rows, :] = (part + LR[n, rows, :].astype(F32)).astype(BF16)
            return carry

        lax.fori_loop(0, 4, for_x, 0)
        if dx:
            lx_in.append(push(remote(LR.at[n], LX.at[n], lx_s.at[n], lx_r.at[n], (c, head))))

    for copy in do_in:
        copy.wait_recv()

    def col_backward(i, carry):
        hh, g = i // 4, lax.rem(i, 4)
        p = PC[i]
        grad = tile(RDO[:, hh, g])
        low = score_gradient(p, nt(grad, tile(REC[2, :, hh, g])))
        SG[0, :, hh, g] = (nn(low, tile(REC[1, :, hh, g])) * SCALE).astype(BF16).reshape(16, 16, 128)
        SG[1, :, hh, g] = (tn(low, tile(REC[0, :, hh, g])) * SCALE).astype(BF16).reshape(16, 16, 128)
        SG[2, :, hh, g] = tn(p.astype(BF16), grad).astype(BF16).reshape(16, 16, 128)
        return carry

    lax.fori_loop(0, 8, col_backward, 0)
    dg_in = []
    stores = []
    for t, dst in enumerate((dqs, dks, dvs)):
        for i, (dy, dz) in enumerate(SEVEN):
            to = grid_peer(dy, dz)
            dg_in.append(push(remote(SG.at[t, to], dst.at[c], dg_s.at[t, i], dg_r.at[t, i], (to, h))))
        copy = pltpu.make_async_copy(SG.at[t, c], dst.at[c], loc.at[11 + t])
        copy.start()
        stores.append(copy)

    def row_cotangent(m, carry):
        rows = pl.ds(pl.multiple_of(m * 256, 256), 256)
        AGR[rows, :] = nt(OG[rows, :], W[pl.ds(0, 256), :]).astype(BF16)
        return carry

    lax.fori_loop(0, 4, row_cotangent, 0)

    def row_backward(i, carry):
        r, hh = i // 2, lax.rem(i, 2)
        lanes = pl.ds(pl.multiple_of(hh * 128, 128), 128)
        for b in range(2):
            n = 256 * (b + 1)
            rows = pl.ds(256 * b, 256)
            seen = pl.ds(0, n)
            p = PR[i, rows, seen]
            grad = AGR[pl.ds(pl.multiple_of(r * 512 + 256 * b, 256), 256), lanes]
            low = score_gradient(p, nt(grad, QKVR[2, i, seen, :]))
            DR[0, i, rows, :] = (nn(low, QKVR[1, i, seen, :]) * SCALE).astype(BF16)
            dk = tn(low, QKVR[0, i, rows, :])
            dv = tn(p.astype(BF16), grad)
            if b == 0:
                dk_first, dv_first = dk, dv
            else:
                DR[1, i, pl.ds(0, 256), :] = ((dk[:256] + dk_first) * SCALE).astype(BF16)
                DR[1, i, pl.ds(256, 256), :] = (dk[256:] * SCALE).astype(BF16)
                DR[2, i, pl.ds(0, 256), :] = (dv[:256] + dv_first).astype(BF16)
                DR[2, i, pl.ds(256, 256), :] = dv[256:].astype(BF16)
        return carry

    lax.fori_loop(0, 4, row_backward, 0)
    for t, dst in enumerate((dqr, dkr, dvr)):
        copy = pltpu.make_async_copy(DR.at[t], dst, loc.at[14 + t])
        copy.start()
        stores.append(copy)

    for copy in p1_in:
        copy.wait_recv()
    p2_in = []
    for half in range(2):
        for d in (1, 2, 3, 0):
            if half == 0:
                other = lax.rem(y + d, 4)
                total = PP[0, other, z].astype(F32)
                dev = (grid_peer(d, 0), h)
            else:
                other = lax.rem(z + d, 4)
                total = PP[1, y, other].astype(F32)
                dev = (grid_peer(0, d), h)
            for k in range(3):
                total = total + R1[half, k, other].astype(F32)
            S2[half, d] = total.astype(BF16)
            if d:
                p2_in.append(
                    push(remote(S2.at[half, d], R2.at[half, d - 1], p2_s.at[half, d - 1], p2_r.at[half, d - 1], dev))
                )

    for copy in lx_in:
        copy.wait_recv()

    def finish(m, carry):
        rows = pl.ds(pl.multiple_of(m * 256, 256), 256)
        total = LR[3, rows, :].astype(F32)
        for k in range(3):
            total = total + LX[k, rows, :].astype(F32)
        LX[0, rows, :] = total.astype(BF16)
        return carry

    lax.fori_loop(0, 4, finish, 0)
    copy = pltpu.make_async_copy(LX.at[0], lay_out, loc.at[17])
    copy.start()
    stores.append(copy)

    for copy in p2_in:
        copy.wait_recv()
    for half in range(2):
        total = S2[half, 0].astype(F32)
        for k in range(3):
            total = total + R2[half, k].astype(F32)
        PG[half] = total.astype(BF16)
        for hh in range(2):
            copy = pltpu.make_async_copy(
                PG.at[half, pl.ds(hh * 128, 128)], pg_out.at[pl.ds((2 * hh + half) * 128, 128)], loc.at[18 + 2 * half + hh]
            )
            copy.start()
            stores.append(copy)

    for copy in dg_in:
        copy.wait_recv()
    for copy in stores:
        copy.wait()
    for copy in sends:
        copy.wait_send()


def on_device(queries, keys, values, out_grad, wo):
    def split(tensor):
        grid = tensor.reshape(2, 16, 4, 8, 2, 2, 128)
        row = grid[:, :, :, :, :, 0].transpose(0, 4, 1, 2, 3, 5).reshape(4, 512, 128)
        strided = grid[:, :, :, :, :, 1].transpose(1, 4, 2, 0, 3, 5).reshape(16, 2, 4, 16, 128)
        return row, strided

    def join(row, strided):
        row = row.reshape(2, 2, 16, 4, 8, 128).transpose(0, 2, 3, 4, 1, 5)
        strided = strided.reshape(16, 2, 4, 2, 8, 128).transpose(3, 0, 2, 4, 1, 5)
        return jnp.stack([row, strided], axis=5).reshape(1024, 4, 128)

    rows, strided = zip(*(split(t) for t in (queries, keys, values)))
    row_shape = jax.ShapeDtypeStruct((4, 512, 128), BF16)
    strided_shape = jax.ShapeDtypeStruct((16, 2, 4, 16, 128), BF16)
    any_spec = pl.BlockSpec(memory_space=pl.ANY)

    def vmem(*shape, dtype=BF16):
        return pltpu.VMEM(shape, dtype)

    def sems(*shape):
        return pltpu.SemaphoreType.DMA(shape)

    out = pl.pallas_call(
        kernel,
        name="layer",
        out_shape=(
            jax.ShapeDtypeStruct((1024, 512), BF16),
            row_shape, row_shape, row_shape,
            strided_shape, strided_shape, strided_shape,
            jax.ShapeDtypeStruct((512, 256), BF16),
        ),
        in_specs=[any_spec] * 8,
        out_specs=[any_spec] * 8,
        scratch_shapes=[
            vmem(512, 4096),
            vmem(1024, 4096),
            vmem(3, 4, 512, 128),
            vmem(3, 16, 2, 4, 16, 128),
            vmem(16, 2, 4, 16, 128),
            vmem(16, 2, 4, 16, 128),
            vmem(16, 2, 4, 16, 128),
            vmem(16, 2, 4, 16, 128),
            vmem(3, 16, 2, 4, 16, 128),
            vmem(8, 256, 256, dtype=F32),
            vmem(4, 512, 512, dtype=F32),
            vmem(1024, 512),
            vmem(512, 1024),
            vmem(2, 16, 4, 8, 256, dtype=F32),
            vmem(1024, 256),
            vmem(2, 4, 4, 256, 256),
            vmem(2, 3, 4, 256, 256),
            vmem(2, 4, 256, 256),
            vmem(2, 3, 256, 256),
            vmem(4, 1024, 512),
            vmem(4, 1024, 512),
            vmem(3, 1024, 512),
            vmem(3, 4, 512, 128),
            vmem(2, 256, 256),
            sems(22),
            sems(3, 15), sems(3, 15),
            sems(15), sems(15),
            sems(15), sems(15),
            sems(3, 15), sems(3, 15),
            sems(6), sems(6),
            sems(9), sems(9),
            sems(9), sems(9),
            sems(2, 3), sems(2, 3),
            sems(2, 3), sems(2, 3),
            sems(4), sems(4),
            sems(3), sems(3),
        ],
        compiler_params=pltpu.CompilerParams(
            collective_id=0, has_side_effects=True, vmem_limit_bytes=63 << 20
        ),
    )(*rows, *strided, out_grad, wo)
    lay, dqr, dkr, dvr, dqs, dks, dvs, pg = out
    return lay, join(dqr, dqs), join(dkr, dks), join(dvr, dvs), pg


def solution(mesh):
    in_specs = (
        P("ctx", "head", None),
        P("ctx", "head", None),
        P("ctx", "head", None),
        P("ctx", None),
        P("head", "ctx"),
    )
    out_specs = (
        P("ctx", "head"),
        P("ctx", "head", None),
        P("ctx", "head", None),
        P("ctx", "head", None),
        P("head", "ctx"),
    )
    return jax.shard_map(
        on_device, mesh=mesh, in_specs=in_specs, out_specs=out_specs, check_vma=False
    )
```

time: 243 us -> 152 us (0.63)
  Pallas kernels: 0 us -> 123 us
  waiting for transfers between devices: 101 us -> 0 us
  matrix products: 53 us -> 0 us
  starting transfers between devices: 37.9 us -> 0 us
  between operations: 14.2 us -> 0.76 us
  local copies, waits for them, and re-layouts: 32.8 us -> 25.3 us
    pallas_call x0 -> x1, Pallas kernels: none -> 123 us  [on_device(): pl.pallas_call(kernel, name='layer', out_shape=(jax.ShapeDtypeStruct((102...]
    reduce_scatter x2 -> x0, waiting for transfers between devices: 58.4 us -> none  [the longest x1 55.8 us: on_device(): lax.psum_scatter(partial_out.astype(jnp.bfloat16), 'head', scatter_dimens...]
    dot_general x14 -> x0, matrix products: 48.4 us -> none  [the longest x1 9.52 us: on_device(): lax.dot_general(flat_attn, out_grad, (((0,), (0,)), ((), ())), preferred_...]
    all_to_all x8 -> x0, waiting for transfers between devices: 41.5 us -> none  [the longest x1 8.75 us: on_device(): lax.all_to_all(strided[0], 'ctx', split_axis=1, concat_axis=0, tiled=True)]
    all_to_all x8 -> x0, starting transfers between devices: 37.6 us -> none  [the longest x1 8.59 us: on_device(): lax.all_to_all(strided[0], 'ctx', split_axis=1, concat_axis=0, tiled=True)]
    slice x1 -> x3, local copies, waits for them, and re-layouts: 1.5 us -> 8.28 us  [split(): grid[:, :, :, :, :, 1].transpose(1, 4, 2, 0, 3, 5)]
    squeeze x4 -> x0, local copies, waits for them, and re-layouts: 5.33 us -> none  [on_device(): strided = tuple((tensor[:, :, :, 1] for tensor in grids))]
    all_to_all x8 -> x0, local copies, waits for them, and re-layouts: 5.08 us -> none  [the longest x1 1.27 us: on_device(): lax.all_to_all(strided[3], 'ctx', split_axis=1, concat_axis=0, tiled=True)]
  transfers between devices with their start and end apart: 11 -> 0, of which waited for: 10 -> 0; matrix products, arithmetic and copies ran while one was open for 37% -> 0% of each run, Pallas kernels for 0% -> 0%
where the time goes in v1:
time: 152 us; the launch traced here: 151 us
  Pallas kernels  123 us (81%)
  local copies, waits for them, and re-layouts  25.3 us (17%)
  other arithmetic  2.43 us (2%)
    pallas_call x1, Pallas kernels, on_device(): pl.pallas_call(kernel, name='layer', out_shape=(jax.ShapeDtypeStruct((102...  123 us
    slice x3, local copies, waits for them, and re-layouts, split(): grid[:, :, :, :, :, 1].transpose(1, 4, 2, 0, 3, 5)  8.28 us
    another operation x3, local copies, waits for them, and re-layouts, join(): return jnp.stack([row, strided], axis=5).reshape(1024, 4, 128)  7.79 us
    unnamed x18, local copies, waits for them, and re-layouts  5.34 us

profile of v1, /device:TPU:1, one launch (start us, length us, event | category | flops | bytes accessed | tf_op | source)
XLA Modules:
  0.0 151.3 jit_solution(6494741809038617956)
XLA Ops:
  0.6 0.0 copy-start.1
  0.6 0.0 copy-start
  0.7 3.7 %fusion.2 = (bf16[2,16,4,8,2,1,128]{6,5,4,3,2,1,0:T(2,128)(2,1)S(1)}, bf16[2,16,4,8,2,1,128]{6,5,4,3,2,1,0:T(2,128)(2,1)S(1)}) fusion(bf16[2,16,4,8,2,2,128]{6,5,4,3,2,1,0:T(2,128)(2,1)} %bitcast.73), kind=kLoop, calls=%fused_computation.11 | loop fusion | bytes 2097152 | tf_op jit(solution)/shard_map/slice | solution.py:394
  4.4 0.9 copy.34
  5.3 0.9 copy.22
  6.2 2.3 %fusion.1 = (bf16[2,16,4,8,2,1,128]{6,5,4,3,2,1,0:T(2,128)(2,1)S(1)}, bf16[2,16,4,8,2,1,128]{6,5,4,3,2,1,0:T(2,128)(2,1)S(1)}) fusion(bf16[2,16,4,8,2,2,128]{6,5,4,3,2,1,0:T(2,128)(2,1)S(1)} %bitcast.74), kind=kLoop, calls=%fused_computation.10 | loop fusion | bytes 2097152 | tf_op jit(solution)/shard_map/slice | solution.py:394
  8.5 0.9 copy.23
  9.4 2.3 %fusion = (bf16[2,16,4,8,2,1,128]{6,5,4,3,2,1,0:T(2,128)(2,1)S(1)}, bf16[2,16,4,8,2,1,128]{6,5,4,3,2,1,0:T(2,128)(2,1)S(1)}) fusion(bf16[2,16,4,8,2,2,128]{6,5,4,3,2,1,0:T(2,128)(2,1)S(1)} %bitcast.75), kind=kLoop, calls=%fused_computation.9 | loop fusion | bytes 2097152 | tf_op jit(solution)/shard_map/slice | solution.py:394
  11.7 1.3 copy_bitcast_fusion
  13.0 0.9 copy.24
  13.9 122.8 %layer.1 = (bf16[1024,512]{1,0:T(8,128)(2,1)}, bf16[4,512,128]{2,1,0:T(8,128)(2,1)}, bf16[4,512,128]{2,1,0:T(8,128)(2,1)}, bf16[4,512,128]{2,1,0:T(8,128)(2,1)},...) custom-call(bf16[4,512,128]{2,1,0:T(8,128)(2,1)} %bitcast.77, ...), custom_call_target="tpu_custom_call" | custom-call | tf_op jit(solution)/shard_map/layer/pallas_call | solution.py:413
  136.7 0.0 copy-start.3
  136.7 0.0 copy-start.4
  136.8 1.3 copy.37
  138.1 1.2 pad_maximum_fusion
  139.3 2.6 %copy.17 = bf16[2,16,4,8,2,2,128]{6,5,4,3,2,1,0:T(2,128)(2,1)} copy(bf16[2,16,4,8,2,2,128]{6,3,0,2,4,1,5:T(8,128)(2,1)S(1)} %pad_maximum_fusion) | data formatting | bytes 2097152 | tf_op jit(solution)/shard_map/stack | solution.py:400
  141.9 1.2 copy.36
  143.1 1.1 pad_maximum_fusion.1
  144.2 2.6 %copy.19 = bf16[2,16,4,8,2,2,128]{6,5,4,3,2,1,0:T(2,128)(2,1)} copy(bf16[2,16,4,8,2,2,128]{6,3,0,2,4,1,5:T(8,128)(2,1)S(1)} %pad_maximum_fusion.1) | data formatting | bytes 2097152 | tf_op jit(solution)/shard_map/stack | solution.py:400
  146.8 0.1 copy.35
  147.0 0.1 pad_maximum_fusion.2
  147.1 2.6 %copy.21 = bf16[2,16,4,8,2,2,128]{6,5,4,3,2,1,0:T(2,128)(2,1)} copy(bf16[2,16,4,8,2,2,128]{6,3,0,2,4,1,5:T(8,128)(2,1)S(1)} %pad_maximum_fusion.2) | data formatting | bytes 2097152 | tf_op jit(solution)/shard_map/stack | solution.py:400
  149.7 1.0 copy.40
  150.6 0.7 copy.41
  (8 shorter events, 0.0 us)
Async XLA Ops:
  0.6 8.8 %copy-start.1 = (bf16[1024,4,128]{2,1,0:T(4,128)(2,1)S(1)}, bf16[1024,4,128]{2,1,0:T(4,128)(2,1)}, u32[]{:S(2)}) copy-start(bf16[1024,4,128]{2,1,0:T(4,128)(2,1)} %param.7) | copy-start | bytes 3145732
  0.6 5.6 %copy-start = (bf16[1024,4,128]{2,1,0:T(4,128)(2,1)S(1)}, bf16[1024,4,128]{2,1,0:T(4,128)(2,1)}, u32[]{:S(2)}) copy-start(bf16[1024,4,128]{2,1,0:T(4,128)(2,1)} %param.6) | copy-start | bytes 3145732
  136.7 10.1 %copy-start.3 = (bf16[4,512,128]{2,1,0:T(8,128)(2,1)S(1)}, bf16[4,512,128]{2,1,0:T(8,128)(2,1)}, u32[]{:S(2)}) copy-start(bf16[4,512,128]{2,1,0:T(8,128)(2,1)} %get-tuple-element.18) | copy-start | bytes 1572868
  136.7 10.2 %copy-start.4 = (bf16[16,2,4,16,128]{4,3,2,1,0:T(8,128)(2,1)S(1)}, bf16[16,2,4,16,128]{4,3,2,1,0:T(8,128)(2,1)}, u32[]{:S(2)}) copy-start(bf16[16,2,4,16,128]{4,3,2,1,0:T(8,128)(2,1)} %get-tuple-element.19) | copy-start | bytes 1572868
  136.7 12.9 %copy-start.2 = (bf16[1024,512]{1,0:T(8,128)(2,1)S(1)}, bf16[1024,512]{1,0:T(8,128)(2,1)}, u32[]{:S(2)}) copy-start(bf16[1024,512]{1,0:T(8,128)(2,1)} %get-tuple-element.34) | copy-start | bytes 3145732
  138.1 12.6 %copy-start.5 = (bf16[512,256]{1,0:T(8,128)(2,1)S(1)}, bf16[512,256]{1,0:T(8,128)(2,1)}, u32[]{:S(2)}) copy-start(bf16[512,256]{1,0:T(8,128)(2,1)} %get-tuple-element.38) | copy-start | bytes 786436

commit v2 on v1

v2 whole, which is shorter than its diff:
```python
import jax
import jax.numpy as jnp
from jax import lax
from jax.experimental import pallas as pl
from jax.experimental.pallas import tpu as pltpu
from jax.sharding import PartitionSpec as P

MESH = pl.DeviceIdType.MESH
BF16 = jnp.bfloat16
F32 = jnp.float32
SCALE = 128 ** -0.5
SEVEN = tuple((dy, dz) for dy in range(4) for dz in range(4) if dy or dz)


def nt(a, b):
    return lax.dot_general(a, b, (((1,), (1,)), ((), ())), preferred_element_type=F32)


def nn(a, b):
    return lax.dot_general(a, b, (((1,), (0,)), ((), ())), preferred_element_type=F32)


def tn(a, b):
    return lax.dot_general(a, b, (((0,), (0,)), ((), ())), preferred_element_type=F32)


def softmax(scores, visible):
    scores = jnp.where(visible, scores * SCALE, -jnp.inf)
    lifted = jnp.exp(scores - jnp.max(scores, axis=-1, keepdims=True))
    return lifted / jnp.sum(lifted, axis=-1, keepdims=True)


def score_gradient(p, dp):
    return (p * (dp - jnp.sum(p * dp, axis=-1, keepdims=True))).astype(BF16)


def kernel(
    q_hbm, k_hbm, v_hbm, og_hbm, wo_hbm,
    lay_out, dq_out, dk_out, dv_out, pg_out,
    RAW, WIDE, QS, RDG,
    W, OG, QKVR, REC, RDO, SO, RO, SDO, SG, PC, PR, ATT, ATTT, AGF, AGR, PP, RL, R1, S2, R2, LS, LR, LX, XR, PG,
    loc, qkv_s, qkv_r, o_s, o_r, do_s, do_r, dg_s, dg_r, w1_s, w1_r, wa_s, wa_r, wb_s, wb_r, wc_s, wc_r,
    p1_s, p1_r, p2_s, p2_r, lp_s, lp_r, lx_s, lx_r,
):
    c = lax.axis_index("ctx")
    h = lax.axis_index("head")
    y, z = c // 4, lax.rem(c, 4)
    x, core = h // 2, lax.rem(h, 2)

    def grid_peer(dy, dz):
        return lax.rem(y + dy, 4) * 4 + lax.rem(z + dz, 4)

    def x_head(dx):
        return lax.rem(x + dx, 4) * 2 + core

    partner = (c, x * 2 + (1 - core))

    def remote(src, dst, ssem, rsem, dev):
        return pltpu.make_async_remote_copy(
            src_ref=src, dst_ref=dst, send_sem=ssem, recv_sem=rsem, device_id=dev, device_id_type=MESH
        )

    sends = []

    def push(copy):
        copy.start()
        sends.append(copy)
        return copy

    own_cols = pl.ds(pl.multiple_of(c * 256, 256), 256)

    loads_q = []
    for t, src in enumerate((q_hbm, k_hbm, v_hbm)):
        copy = pltpu.make_async_copy(src, RAW.at[t], loc.at[t])
        copy.start()
        loads_q.append(copy)
    loads_w = []
    for slot, j in enumerate((0, 2, 1, 3)):
        copy = pltpu.make_async_copy(
            wo_hbm.at[pl.ds(j * 128, 128)], W.at[pl.ds(slot * 128, 128), own_cols], loc.at[3 + slot]
        )
        copy.start()
        loads_w.append(copy)
    load_og = pltpu.make_async_copy(og_hbm, OG, loc.at[7])
    load_og.start()

    barrier = pltpu.get_barrier_semaphore()
    for dy, dz in SEVEN:
        pl.semaphore_signal(barrier, inc=1, device_id=(grid_peer(dy, dz), h), device_id_type=MESH)
    for dx in range(1, 4):
        pl.semaphore_signal(barrier, inc=1, device_id=(c, x_head(dx)), device_id_type=MESH)
    pl.semaphore_signal(barrier, inc=1, device_id=partner, device_id_type=MESH)

    def unpack(t):
        loads_q[t].wait()

        def widen(m, carry):
            rows = pl.ds(pl.multiple_of(m * 512, 512), 512)
            WIDE[t, rows, :] = RAW[t, rows, :].astype(F32)
            return carry

        lax.fori_loop(0, 8, widen, 0)

        def strided(m, carry):
            for hh in range(2):
                both = []
                for r in range(2):
                    first = r * 2048 + 2 * hh + 1 + m * 512
                    both.append(WIDE[t, pl.ds(first, 128, stride=4), :].reshape(4, 4, 8, 128))
                QS[t, pl.ds(m * 4, 4), hh] = jnp.concatenate(both, axis=2).astype(BF16)
            return carry

        lax.fori_loop(0, 4, strided, 0)

    unpack(0)
    for copy in loads_w:
        copy.wait()
    pl.semaphore_wait(barrier, 19)

    w_own = W.at[:, own_cols]
    wz, wy = [], []
    for d in range(1, 4):
        wz.append(push(remote(w_own, w_own, w1_s.at[d - 1], w1_r.at[d - 1], (grid_peer(0, d), h))))
        wy.append(push(remote(w_own, w_own, w1_s.at[2 + d], w1_r.at[2 + d], (grid_peer(d, 0), h))))

    qkv_in = []

    def send_strided(t):
        for i, (dy, dz) in enumerate(SEVEN):
            to = grid_peer(dy, dz)
            qkv_in.append(push(remote(QS.at[t, to], REC.at[t, c], qkv_s.at[t, i], qkv_r.at[t, i], (to, h))))
        REC[t, c] = QS[t, c]

    send_strided(0)
    unpack(1)
    send_strided(1)
    unpack(2)
    send_strided(2)

    def w_block(first, size, owner):
        return W.at[pl.ds(first, size), pl.ds(pl.multiple_of(owner * 256, 256), 256)]

    wa = [[None] * 2 for _ in range(3)]
    wb = [[None] * 2 for _ in range(3)]

    def spread_w():
        for d in range(1, 4):
            wz[d - 1].wait_recv()
            block = w_block(0, 256, grid_peer(0, 4 - d))
            for k, e in enumerate((1, 3)):
                wa[d - 1][k] = push(
                    remote(block, block, wa_s.at[d - 1, k], wa_r.at[d - 1, k], (grid_peer(e, 0), h))
                )
            wy[d - 1].wait_recv()
            block = w_block(256, 256, grid_peer(4 - d, 0))
            for k, e in enumerate((1, 3)):
                wb[d - 1][k] = push(
                    remote(block, block, wb_s.at[d - 1, k], wb_r.at[d - 1, k], (grid_peer(0, e), h))
                )

    wc = []

    def relay_w():
        for d in range(1, 4):
            for k, e in enumerate((1, 3)):
                wa[d - 1][k].wait_recv()
                block = w_block(128 * k, 128, grid_peer(4 - e, 4 - d))
                wc.append(push(remote(block, block, wc_s.at[0, d - 1, k], wc_r.at[0, d - 1, k], (grid_peer(e, 0), h))))
                wb[d - 1][k].wait_recv()
                block = w_block(256 + 128 * k, 128, grid_peer(4 - d, 4 - e))
                wc.append(push(remote(block, block, wc_s.at[1, d - 1, k], wc_r.at[1, d - 1, k], (grid_peer(0, e), h))))

    def unpack_rows(m, carry):
        for t in range(3):
            for hh in range(2):
                rows = WIDE[t, pl.ds(m * 512 + 2 * hh, 128, stride=4), :].astype(BF16)
                QKVR[t, (m // 4) * 2 + hh, pl.ds(pl.multiple_of(lax.rem(m, 4) * 128, 128), 128), :] = rows
        return carry

    lax.fori_loop(0, 8, unpack_rows, 0)

    def causal(rows, cols, first):
        return (
            lax.broadcasted_iota(jnp.int32, (rows, cols), 0) + first
            >= lax.broadcasted_iota(jnp.int32, (rows, cols), 1)
        )

    def row_forward(i, carry):
        r, hh = i // 2, lax.rem(i, 2)
        lanes = pl.ds(pl.multiple_of(hh * 128, 128), 128)
        for b in range(2):
            n = 256 * (b + 1)
            q = QKVR[0, i, pl.ds(256 * b, 256), :]
            p = softmax(nt(q, QKVR[1, i, pl.ds(0, n), :]), causal(256, n, 256 * b))
            PR[i, pl.ds(256 * b, 256), pl.ds(0, n)] = p
            o = nn(p.astype(BF16), QKVR[2, i, pl.ds(0, n), :])
            rows = pl.ds(pl.multiple_of(r * 512 + 256 * b, 256), 256)
            ATT[rows, lanes] = o.astype(BF16)
            ATTT[lanes, rows] = o.T.astype(BF16)
        return carry

    lax.fori_loop(0, 4, row_forward, 0)

    def projection(half):
        def one(n, carry):
            cols = pl.ds(pl.multiple_of(n * 256, 256), 256)
            part = nn(ATTT[pl.ds(256 * half, 256), :], OG[:, cols])
            for q in range(2):
                PP[2 * half + q, n // 4, lax.rem(n, 4)] = part[128 * q : 128 * q + 128].astype(BF16)
            return carry

        lax.fori_loop(0, 16, one, 0)

    spread_w()
    load_og.wait()
    projection(0)

    first_half, second_half = pl.ds(0, 2), pl.ds(2, 2)

    def group(q, d, part):
        if q % 2 == 0:
            return PP.at[q, part, lax.rem(z + d, 4)]
        return PP.at[q, lax.rem(y + d, 4), part]

    def along(q, d, second=False):
        return (grid_peer(0, d) if (q % 2 == 0) != second else grid_peer(d, 0), h)

    pr_in, p1_in, p2_in = [None] * 4, [None] * 4, [None] * 4

    def reduce_start(q):
        pr_in[q] = [
            push(remote(group(q, 2, first_half), RL.at[q, 0], p1_s.at[q, 0], p1_r.at[q, 0], along(q, 1))),
            push(remote(group(q, 2, second_half), RL.at[q, 1], p1_s.at[q, 1], p1_r.at[q, 1], along(q, 3))),
        ]
        p1_in[q] = [
            push(remote(group(q, 1, second_half), R1.at[q, 0, second_half], p1_s.at[q, 2], p1_r.at[q, 2], along(q, 1))),
            push(remote(group(q, 3, first_half), R1.at[q, 1, first_half], p1_s.at[q, 3], p1_r.at[q, 3], along(q, 3))),
        ]

    def reduce_pass(q):
        for k, (d, part) in enumerate(((1, first_half), (3, second_half))):
            pr_in[q][k].wait_recv()
            mine = group(q, d, part)
            mine[...] = (mine[...].astype(F32) + RL[q, k].astype(F32)).astype(BF16)
            p1_in[q].append(
                push(remote(mine, R1.at[q, k, part], p1_s.at[q, 4 + k], p1_r.at[q, 4 + k], along(q, d)))
            )

    def reduce_middle(q):
        for copy in p1_in[q]:
            copy.wait_recv()
        p2_in[q] = []
        for d in (2, 1, 3, 0):
            if q % 2 == 0:
                other = lax.rem(y + d, 4)
                mine = PP[q, other, z]
            else:
                other = lax.rem(z + d, 4)
                mine = PP[q, y, other]
            total = mine.astype(F32) + R1[q, 0, other].astype(F32) + R1[q, 1, other].astype(F32)
            S2[q, d] = total.astype(BF16)
            if d:
                p2_in[q].append(
                    push(remote(S2.at[q, d], R2.at[q, d - 1], p2_s.at[q, d - 1], p2_r.at[q, d - 1], along(q, d, True)))
                )

    def reduce_end(q):
        for copy in p2_in[q]:
            copy.wait_recv()
        total = S2[q, 0].astype(F32)
        for k in range(3):
            total = total + R2[q, k].astype(F32)
        PG[q] = total.astype(BF16)
        copy = pltpu.make_async_copy(PG.at[q], pg_out.at[pl.ds((2 * (q % 2) + q // 2) * 128, 128)], loc.at[12 + q])
        copy.start()
        stores.append(copy)

    for copy in qkv_in:
        copy.wait_recv()
    ii = lax.broadcasted_iota(jnp.int32, (256, 256), 0)
    jj = lax.broadcasted_iota(jnp.int32, (256, 256), 1)

    def tile(ref):
        return ref.reshape(256, 128)

    def col_forward(i, carry):
        hh, g = i // 4, lax.rem(i, 4)
        visible = (lax.rem(ii, 8) == lax.rem(jj, 8)) & (ii >= jj)
        p = softmax(nt(tile(REC[0, :, hh, g]), tile(REC[1, :, hh, g])), visible)
        PC[i] = p
        o = nn(p.astype(BF16), tile(REC[2, :, hh, g]))
        SO[:, hh, g] = o.astype(BF16).reshape(16, 16, 128)
        return carry

    lax.fori_loop(0, 8, col_forward, 0, unroll=2)
    o_in = []
    for i, (dy, dz) in enumerate(SEVEN):
        to = grid_peer(dy, dz)
        o_in.append(push(remote(SO.at[to], RO.at[c], o_s.at[i], o_r.at[i], (to, h))))
    RO[c] = SO[c]

    relay_w()
    reduce_start(0)
    reduce_start(1)

    for copy in o_in:
        copy.wait_recv()
    for hh in range(2):
        for g in range(4):
            block = RO[:, hh, g].astype(F32)
            for r in range(2):
                AGF[r, :, g, :, pl.ds(hh * 128, 128)] = block[:, 8 * r : 8 * r + 8, :]

    def place(m, carry):
        block = AGF[m // 2, pl.ds(pl.multiple_of(lax.rem(m, 2) * 8, 8), 8)].reshape(256, 256)
        rows = pl.ds(pl.multiple_of(m * 256, 256), 256)
        ATT[rows, pl.ds(256, 256)] = block.astype(BF16)
        ATTT[pl.ds(256, 256), rows] = block.T.astype(BF16)
        return carry

    lax.fori_loop(0, 4, place, 0)
    projection(1)

    for copy in wc:
        copy.wait_recv()

    def strided_cotangent(m, carry):
        rows = pl.ds(pl.multiple_of(m * 256, 256), 256)
        part = nt(OG[rows, :], W[pl.ds(256, 256), :])
        AGF[m // 2, pl.ds(pl.multiple_of(lax.rem(m, 2) * 8, 8), 8)] = part.reshape(8, 4, 8, 256)
        return carry

    lax.fori_loop(0, 4, strided_cotangent, 0)
    for hh in range(2):
        for g in range(4):
            lanes = pl.ds(hh * 128, 128)
            both = jnp.concatenate([AGF[0, :, g, :, lanes], AGF[1, :, g, :, lanes]], axis=1)
            SDO[:, hh, g] = both.astype(BF16)
    do_in = []
    for i, (dy, dz) in enumerate(SEVEN):
        to = grid_peer(dy, dz)
        do_in.append(push(remote(SDO.at[to], RDO.at[c], do_s.at[i], do_r.at[i], (to, h))))
    RDO[c] = SDO[c]
    reduce_start(2)
    reduce_start(3)
    reduce_pass(0)
    reduce_pass(1)

    def partial_out(m, head):
        rows = pl.ds(pl.multiple_of(m * 256, 256), 256)
        cols = pl.ds(pl.multiple_of(head * 512, 512), 512)
        return rows, nn(ATT[rows, :], W[:, cols])

    order = (2, 1, 3, 0)
    lp_in = [None] * 4

    def to_partner(n):
        head = lax.rem(x + order[n], 4) * 2 + (1 - core)

        def for_partner(m, carry):
            rows, part = partial_out(m, head)
            LS[n, rows, :] = part.astype(BF16)
            return carry

        lax.fori_loop(0, 4, for_partner, 0)
        lp_in[n] = push(remote(LS.at[n], LR.at[n], lp_s.at[n], lp_r.at[n], partner))

    def to_x(n):
        head = x_head(order[n])
        lp_in[n].wait_recv()

        def for_x(m, carry):
            rows, part = partial_out(m, head)
            LR[n, rows, :] = (part + LR[n, rows, :].astype(F32)).astype(BF16)
            return carry

        lax.fori_loop(0, 4, for_x, 0)

    lower, upper = pl.ds(0, 512), pl.ds(512, 512)
    ahead, behind = (c, x_head(1)), (c, x_head(3))

    def add_passing(n, k, rows):
        relay[k].wait_recv()
        LR[n, rows, :] = (LR[n, rows, :].astype(F32) + XR[k].astype(F32)).astype(BF16)

    to_partner(0)
    to_partner(1)
    to_x(0)
    relay = [
        push(remote(LR.at[0, lower], XR.at[0], lx_s.at[0], lx_r.at[0], ahead)),
        push(remote(LR.at[0, upper], XR.at[1], lx_s.at[1], lx_r.at[1], behind)),
    ]
    to_partner(2)
    to_x(1)
    lx_in = [push(remote(LR.at[1, upper], LX.at[0, upper], lx_s.at[2], lx_r.at[2], ahead))]
    to_partner(3)
    to_x(2)
    lx_in.append(push(remote(LR.at[2, lower], LX.at[1, lower], lx_s.at[3], lx_r.at[3], behind)))

    for copy in do_in:
        copy.wait_recv()

    def col_backward(i, carry):
        hh, g = i // 4, lax.rem(i, 4)
        p = PC[i]
        grad = tile(RDO[:, hh, g])
        low = score_gradient(p, nt(grad, tile(REC[2, :, hh, g])))
        SG[0, :, hh, g] = (nn(low, tile(REC[1, :, hh, g])) * SCALE).astype(BF16).reshape(16, 16, 128)
        SG[1, :, hh, g] = (tn(low, tile(REC[0, :, hh, g])) * SCALE).astype(BF16).reshape(16, 16, 128)
        SG[2, :, hh, g] = tn(p.astype(BF16), grad).astype(BF16).reshape(16, 16, 128)
        return carry

    lax.fori_loop(0, 8, col_backward, 0, unroll=2)
    reduce_pass(2)
    reduce_pass(3)
    dg_in = []
    stores = []
    for t in range(3):
        for i, (dy, dz) in enumerate(SEVEN):
            to = grid_peer(dy, dz)
            dg_in.append(push(remote(SG.at[t, to], RDG.at[t, c], dg_s.at[t, i], dg_r.at[t, i], (to, h))))
        RDG[t, c] = SG[t, c]

    to_x(3)
    add_passing(1, 0, lower)
    lx_in.append(push(remote(LR.at[1, lower], LX.at[0, lower], lx_s.at[4], lx_r.at[4], ahead)))
    add_passing(2, 1, upper)
    lx_in.append(push(remote(LR.at[2, upper], LX.at[1, upper], lx_s.at[5], lx_r.at[5], behind)))

    reduce_middle(0)
    reduce_middle(1)
    reduce_middle(2)
    reduce_middle(3)

    def row_cotangent(m, carry):
        rows = pl.ds(pl.multiple_of(m * 256, 256), 256)
        AGR[rows, :] = nt(OG[rows, :], W[pl.ds(0, 256), :]).astype(BF16)
        return carry

    lax.fori_loop(0, 4, row_cotangent, 0)

    def row_backward(i, carry):
        r, hh = i // 2, lax.rem(i, 2)
        lanes = pl.ds(pl.multiple_of(hh * 128, 128), 128)
        for b in range(2):
            n = 256 * (b + 1)
            rows = pl.ds(256 * b, 256)
            seen = pl.ds(0, n)
            p = PR[i, rows, seen]
            grad = AGR[pl.ds(pl.multiple_of(r * 512 + 256 * b, 256), 256), lanes]
            low = score_gradient(p, nt(grad, QKVR[2, i, seen, :]))
            first = r * 2048 + 2 * hh
            WIDE[0, pl.ds(first + 1024 * b, 256, stride=4), :] = nn(low, QKVR[1, i, seen, :]) * SCALE
            dk = tn(low, QKVR[0, i, rows, :])
            dv = tn(p.astype(BF16), grad)
            if b == 0:
                dk_first, dv_first = dk, dv
            else:
                WIDE[1, pl.ds(first, 256, stride=4), :] = (dk[:256] + dk_first) * SCALE
                WIDE[1, pl.ds(first + 1024, 256, stride=4), :] = dk[256:] * SCALE
                WIDE[2, pl.ds(first, 256, stride=4), :] = dv[:256] + dv_first
                WIDE[2, pl.ds(first + 1024, 256, stride=4), :] = dv[256:]
        return carry

    lax.fori_loop(0, 4, row_backward, 0)

    for copy in lx_in:
        copy.wait_recv()

    def finish(m, carry):
        rows = pl.ds(pl.multiple_of(m * 256, 256), 256)
        total = LR[3, rows, :].astype(F32) + LX[0, rows, :].astype(F32) + LX[1, rows, :].astype(F32)
        LX[0, rows, :] = total.astype(BF16)
        return carry

    lax.fori_loop(0, 4, finish, 0)
    copy = pltpu.make_async_copy(LX.at[0], lay_out, loc.at[11])
    copy.start()
    stores.append(copy)

    for q in range(4):
        reduce_end(q)

    for t, dst in enumerate((dq_out, dk_out, dv_out)):
        for copy in dg_in[15 * t : 15 * t + 15]:
            copy.wait_recv()

        def spread(m, carry, t=t):
            for hh in range(2):
                block = RDG[t, pl.ds(m * 4, 4), hh].astype(F32)
                for r in range(2):
                    first = r * 2048 + 2 * hh + 1 + m * 512
                    WIDE[t, pl.ds(first, 128, stride=4), :] = block[:, :, 8 * r : 8 * r + 8, :].reshape(128, 128)
            return carry

        lax.fori_loop(0, 4, spread, 0)

        def narrow(m, carry, t=t):
            rows = pl.ds(pl.multiple_of(m * 512, 512), 512)
            RAW[t, rows, :] = WIDE[t, rows, :].astype(BF16)
            return carry

        lax.fori_loop(0, 8, narrow, 0)
        copy = pltpu.make_async_copy(RAW.at[t], dst, loc.at[8 + t])
        copy.start()
        stores.append(copy)
    for copy in stores:
        copy.wait()
    for copy in sends:
        copy.wait_send()


def on_device(queries, keys, values, out_grad, wo):
    flat = tuple(t.reshape(4096, 128) for t in (queries, keys, values))
    flat_shape = jax.ShapeDtypeStruct((4096, 128), BF16)
    any_spec = pl.BlockSpec(memory_space=pl.ANY)

    def vmem(*shape, dtype=BF16):
        return pltpu.VMEM(shape, dtype)

    def sems(*shape):
        return pltpu.SemaphoreType.DMA(shape)

    out = pl.pallas_call(
        kernel,
        name="layer",
        out_shape=(
            jax.ShapeDtypeStruct((1024, 512), BF16),
            flat_shape, flat_shape, flat_shape,
            jax.ShapeDtypeStruct((512, 256), BF16),
        ),
        in_specs=[any_spec] * 5,
        out_specs=[any_spec] * 5,
        scratch_shapes=[
            vmem(3, 4096, 128),
            vmem(3, 4096, 128, dtype=F32),
            vmem(3, 16, 2, 4, 16, 128),
            vmem(3, 16, 2, 4, 16, 128),
            vmem(512, 4096),
            vmem(1024, 4096),
            vmem(3, 4, 512, 128),
            vmem(3, 16, 2, 4, 16, 128),
            vmem(16, 2, 4, 16, 128),
            vmem(16, 2, 4, 16, 128),
            vmem(16, 2, 4, 16, 128),
            vmem(16, 2, 4, 16, 128),
            vmem(3, 16, 2, 4, 16, 128),
            vmem(8, 256, 256, dtype=F32),
            vmem(4, 512, 512, dtype=F32),
            vmem(1024, 512),
            vmem(512, 1024),
            vmem(2, 16, 4, 8, 256, dtype=F32),
            vmem(1024, 256),
            vmem(4, 4, 4, 128, 256),
            vmem(4, 2, 2, 128, 256),
            vmem(4, 2, 4, 128, 256),
            vmem(4, 4, 128, 256),
            vmem(4, 3, 128, 256),
            vmem(4, 1024, 512),
            vmem(4, 1024, 512),
            vmem(2, 1024, 512),
            vmem(2, 512, 512),
            vmem(4, 128, 256),
            sems(16),
            sems(3, 15), sems(3, 15),
            sems(15), sems(15),
            sems(15), sems(15),
            sems(3, 15), sems(3, 15),
            sems(6), sems(6),
            sems(3, 2), sems(3, 2),
            sems(3, 2), sems(3, 2),
            sems(2, 3, 2), sems(2, 3, 2),
            sems(4, 6), sems(4, 6),
            sems(4, 3), sems(4, 3),
            sems(4), sems(4),
            sems(6), sems(6),
        ],
        compiler_params=pltpu.CompilerParams(
            collective_id=0, has_side_effects=True, vmem_limit_bytes=63 << 20
        ),
    )(*flat, out_grad, wo)
    lay, dq, dk, dv, pg = out
    return lay, *(t.reshape(1024, 4, 128) for t in (dq, dk, dv)), pg


def solution(mesh):
    in_specs = (
        P("ctx", "head", None),
        P("ctx", "head", None),
        P("ctx", "head", None),
        P("ctx", None),
        P("head", "ctx"),
    )
    out_specs = (
        P("ctx", "head"),
        P("ctx", "head", None),
        P("ctx", "head", None),
        P("ctx", "head", None),
        P("head", "ctx"),
    )
    return jax.shard_map(
        on_device, mesh=mesh, in_specs=in_specs, out_specs=out_specs, check_vma=False
    )
```

time: 152 us -> 122 us (0.80)
  local copies, waits for them, and re-layouts: 25.3 us -> 10.7 us
  Pallas kernels: 123 us -> 110 us
  other arithmetic: 2.43 us -> 0 us
    pallas_call x1, Pallas kernels: 123 us -> 110 us  [on_device(): pl.pallas_call(kernel, name='layer', out_shape=(jax.ShapeDtypeStruct((102...]
    slice x3 -> x0, local copies, waits for them, and re-layouts: 8.28 us -> none  [split(): grid[:, :, :, :, :, 1].transpose(1, 4, 2, 0, 3, 5)]
    another operation x3 -> x0, local copies, waits for them, and re-layouts: 7.79 us -> none  [join(): return jnp.stack([row, strided], axis=5).reshape(1024, 4, 128)]
    unnamed x18 -> x7, local copies, waits for them, and re-layouts: 5.34 us -> 10.7 us
    reshape x4 -> x0, local copies, waits for them, and re-layouts: 3.93 us -> none  [the longest x3 2.63 us: join(): row = row.reshape(2, 2, 16, 4, 8, 128).transpose(0, 2, 3, 4, 1, 5)]
    another operation x3 -> x0, other arithmetic: 2.43 us -> none  [join(): return jnp.stack([row, strided], axis=5).reshape(1024, 4, 128)]
where the time goes in v2:
time: 122 us
  Pallas kernels  110 us (90%)
  local copies, waits for them, and re-layouts  10.7 us (9%)
    pallas_call x1, Pallas kernels, on_device(): pl.pallas_call(kernel, name='layer', out_shape=(jax.ShapeDtypeStruct((102...  110 us
    unnamed x7, local copies, waits for them, and re-layouts  10.7 us

profile of v2, /device:TPU:1, one launch (start us, length us, event | category | flops | bytes accessed | tf_op | source)
XLA Modules:
  0.0 121.7 jit_solution(2978737738714245981)
XLA Ops:
  0.6 110.4 %layer.1 = (bf16[1024,512]{1,0:T(8,128)(2,1)}, bf16[4096,128]{1,0:T(8,128)(2,1)}, bf16[4096,128]{1,0:T(8,128)(2,1)}, bf16[4096,128]{1,0:T(8,128)(2,1)}, bf16[512,256]{1,0:T(8,128)(2,1)}) custom-call(bf16[4096,128]{1,0:T(8,128)(2,1)} %bitcast.6, bf16[4096,128]{1,0:T(8,128)(2,1)} %bitcast.7, bf16[4096,128]{1,0:T(8,128)(2,1)} %bitcast.8, ...), custom_call_target="tpu_custom_call" | custom-call | tf_op jit(solution)/shard_map/layer/pallas_call | solution.py:524
  111.0 0.0 copy-start
  111.0 2.3 %copy.15 = bf16[1024,512]{1,0:T(8,128)(2,1)} copy(bf16[1024,512]{1,0:T(8,128)(2,1)} %get-tuple-element.20) | data formatting | bytes 2097152
  113.3 2.6 %copy.16 = bf16[1024,4,128]{2,1,0:T(4,128)(2,1)} copy(bf16[1024,4,128]{2,1,0:T(4,128)(2,1)} %bitcast.11) | data formatting | bytes 2097152
  115.9 2.6 %copy.17 = bf16[1024,4,128]{2,1,0:T(4,128)(2,1)} copy(bf16[1024,4,128]{2,1,0:T(4,128)(2,1)} %bitcast.10) | data formatting | bytes 2097152
  118.4 2.6 %copy.18 = bf16[1024,4,128]{2,1,0:T(4,128)(2,1)} copy(bf16[1024,4,128]{2,1,0:T(4,128)(2,1)} %bitcast.9) | data formatting | bytes 2097152
  121.0 0.0 copy-done
  121.0 0.7 copy.19
Async XLA Ops:
  111.0 10.0 %copy-start = (bf16[512,256]{1,0:T(8,128)(2,1)S(1)}, bf16[512,256]{1,0:T(8,128)(2,1)}, u32[]{:S(2)}) copy-start(bf16[512,256]{1,0:T(8,128)(2,1)} %get-tuple-element.24) | copy-start | bytes 786436

commit v3 on v2

--- a/solution.py
+++ b/solution.py
@@ -37,8 +37,8 @@
 def kernel(
     q_hbm, k_hbm, v_hbm, og_hbm, wo_hbm,
     lay_out, dq_out, dk_out, dv_out, pg_out,
-    RAW, WIDE, QS, RDG,
-    W, OG, QKVR, REC, RDO, SO, RO, SDO, SG, PC, PR, ATT, ATTT, AGF, AGR, PP, RL, R1, S2, R2, LS, LR, LX, XR, PG,
+    WIDE, QS, RDG,
+    W, OG, QKVR, REC, RDO, SO, RO, PC, PR, ATT, ATTT, AGF, AGR, PP, RL, R1, S2, R2, LS, LR, LX, XR,
     loc, qkv_s, qkv_r, o_s, o_r, do_s, do_r, dg_s, dg_r, w1_s, w1_r, wa_s, wa_r, wb_s, wb_r, wc_s, wc_r,
     p1_s, p1_r, p2_s, p2_r, lp_s, lp_r, lx_s, lx_r,
 ):
@@ -67,11 +67,17 @@
         sends.append(copy)
         return copy
 
+    def drain(copies):
+        for copy in copies:
+            copy.wait_send()
+            sends[:] = [other for other in sends if other is not copy]
+
+    flat_out = (dq_out, dk_out, dv_out)
     own_cols = pl.ds(pl.multiple_of(c * 256, 256), 256)
 
     loads_q = []
     for t, src in enumerate((q_hbm, k_hbm, v_hbm)):
-        copy = pltpu.make_async_copy(src, RAW.at[t], loc.at[t])
+        copy = pltpu.make_async_copy(src, flat_out[t], loc.at[t])
         copy.start()
         loads_q.append(copy)
     loads_w = []
@@ -96,7 +102,7 @@
 
         def widen(m, carry):
             rows = pl.ds(pl.multiple_of(m * 512, 512), 512)
-            WIDE[t, rows, :] = RAW[t, rows, :].astype(F32)
+            WIDE[t, rows, :] = flat_out[t][rows, :].astype(F32)
             return carry
 
         lax.fori_loop(0, 8, widen, 0)
@@ -270,10 +276,7 @@
         total = S2[q, 0].astype(F32)
         for k in range(3):
             total = total + R2[q, k].astype(F32)
-        PG[q] = total.astype(BF16)
-        copy = pltpu.make_async_copy(PG.at[q], pg_out.at[pl.ds((2 * (q % 2) + q // 2) * 128, 128)], loc.at[12 + q])
-        copy.start()
-        stores.append(copy)
+        pg_out[pl.ds((2 * (q % 2) + q // 2) * 128, 128), :] = total.astype(BF16)
 
     for copy in qkv_in:
         copy.wait_recv()
@@ -331,16 +334,17 @@
         return carry
 
     lax.fori_loop(0, 4, strided_cotangent, 0)
+    drain(o_in)
     for hh in range(2):
         for g in range(4):
             lanes = pl.ds(hh * 128, 128)
             both = jnp.concatenate([AGF[0, :, g, :, lanes], AGF[1, :, g, :, lanes]], axis=1)
-            SDO[:, hh, g] = both.astype(BF16)
+            SO[:, hh, g] = both.astype(BF16)
     do_in = []
     for i, (dy, dz) in enumerate(SEVEN):
         to = grid_peer(dy, dz)
-        do_in.append(push(remote(SDO.at[to], RDO.at[c], do_s.at[i], do_r.at[i], (to, h))))
-    RDO[c] = SDO[c]
+        do_in.append(push(remote(SO.at[to], RDO.at[c], do_s.at[i], do_r.at[i], (to, h))))
+    RDO[c] = SO[c]
     reduce_start(2)
     reduce_start(3)
     reduce_pass(0)
@@ -405,21 +409,21 @@
         p = PC[i]
         grad = tile(RDO[:, hh, g])
         low = score_gradient(p, nt(grad, tile(REC[2, :, hh, g])))
-        SG[0, :, hh, g] = (nn(low, tile(REC[1, :, hh, g])) * SCALE).astype(BF16).reshape(16, 16, 128)
-        SG[1, :, hh, g] = (tn(low, tile(REC[0, :, hh, g])) * SCALE).astype(BF16).reshape(16, 16, 128)
-        SG[2, :, hh, g] = tn(p.astype(BF16), grad).astype(BF16).reshape(16, 16, 128)
-        return carry
-
+        QS[0, :, hh, g] = (nn(low, tile(REC[1, :, hh, g])) * SCALE).astype(BF16).reshape(16, 16, 128)
+        QS[1, :, hh, g] = (tn(low, tile(REC[0, :, hh, g])) * SCALE).astype(BF16).reshape(16, 16, 128)
+        QS[2, :, hh, g] = tn(p.astype(BF16), grad).astype(BF16).reshape(16, 16, 128)
+        return carry
+
+    drain(qkv_in)
     lax.fori_loop(0, 8, col_backward, 0, unroll=2)
     reduce_pass(2)
     reduce_pass(3)
     dg_in = []
-    stores = []
     for t in range(3):
         for i, (dy, dz) in enumerate(SEVEN):
             to = grid_peer(dy, dz)
-            dg_in.append(push(remote(SG.at[t, to], RDG.at[t, c], dg_s.at[t, i], dg_r.at[t, i], (to, h))))
-        RDG[t, c] = SG[t, c]
+            dg_in.append(push(remote(QS.at[t, to], RDG.at[t, c], dg_s.at[t, i], dg_r.at[t, i], (to, h))))
+        RDG[t, c] = QS[t, c]
 
     to_x(3)
     add_passing(1, 0, lower)
@@ -464,24 +468,10 @@
 
     lax.fori_loop(0, 4, row_backward, 0)
 
-    for copy in lx_in:
-        copy.wait_recv()
-
-    def finish(m, carry):
-        rows = pl.ds(pl.multiple_of(m * 256, 256), 256)
-        total = LR[3, rows, :].astype(F32) + LX[0, rows, :].astype(F32) + LX[1, rows, :].astype(F32)
-        LX[0, rows, :] = total.astype(BF16)
-        return carry
-
-    lax.fori_loop(0, 4, finish, 0)
-    copy = pltpu.make_async_copy(LX.at[0], lay_out, loc.at[11])
-    copy.start()
-    stores.append(copy)
-
     for q in range(4):
         reduce_end(q)
 
-    for t, dst in enumerate((dq_out, dk_out, dv_out)):
+    for t in range(3):
         for copy in dg_in[15 * t : 15 * t + 15]:
             copy.wait_recv()
 
@@ -497,22 +487,36 @@
 
         def narrow(m, carry, t=t):
             rows = pl.ds(pl.multiple_of(m * 512, 512), 512)
-            RAW[t, rows, :] = WIDE[t, rows, :].astype(BF16)
+            flat_out[t][rows, :] = WIDE[t, rows, :].astype(BF16)
             return carry
 
         lax.fori_loop(0, 8, narrow, 0)
-        copy = pltpu.make_async_copy(RAW.at[t], dst, loc.at[8 + t])
-        copy.start()
-        stores.append(copy)
-    for copy in stores:
-        copy.wait()
+    for copy in lx_in:
+        copy.wait_recv()
+
+    def finish(m, carry):
+        rows = pl.ds(pl.multiple_of(m * 256, 256), 256)
+        total = LR[3, rows, :].astype(F32) + LX[0, rows, :].astype(F32) + LX[1, rows, :].astype(F32)
+        lay_out[rows, :] = total.astype(BF16)
+        return carry
+
+    lax.fori_loop(0, 4, finish, 0)
     for copy in sends:
         copy.wait_send()
 
 
+def store(*refs):
+    done = refs[10]
+    copies = [pltpu.make_async_copy(refs[i], refs[5 + i], done.at[i]) for i in range(5)]
+    for copy in copies:
+        copy.start()
+    for copy in copies:
+        copy.wait()
+
+
 def on_device(queries, keys, values, out_grad, wo):
     flat = tuple(t.reshape(4096, 128) for t in (queries, keys, values))
-    flat_shape = jax.ShapeDtypeStruct((4096, 128), BF16)
+    flat_shape = pltpu.VMEM((4096, 128), BF16)
     any_spec = pl.BlockSpec(memory_space=pl.ANY)
 
     def vmem(*shape, dtype=BF16):
@@ -525,14 +529,13 @@
         kernel,
         name="layer",
         out_shape=(
-            jax.ShapeDtypeStruct((1024, 512), BF16),
+            pltpu.VMEM((1024, 512), BF16),
             flat_shape, flat_shape, flat_shape,
-            jax.ShapeDtypeStruct((512, 256), BF16),
+            pltpu.VMEM((512, 256), BF16),
         ),
         in_specs=[any_spec] * 5,
-        out_specs=[any_spec] * 5,
+        out_specs=[pl.BlockSpec(memory_space=pltpu.VMEM)] * 5,
         scratch_shapes=[
-            vmem(3, 4096, 128),
             vmem(3, 4096, 128, dtype=F32),
             vmem(3, 16, 2, 4, 16, 128),
             vmem(3, 16, 2, 4, 16, 128),
@@ -543,8 +546,6 @@
             vmem(16, 2, 4, 16, 128),
             vmem(16, 2, 4, 16, 128),
             vmem(16, 2, 4, 16, 128),
-            vmem(16, 2, 4, 16, 128),
-            vmem(3, 16, 2, 4, 16, 128),
             vmem(8, 256, 256, dtype=F32),
             vmem(4, 512, 512, dtype=F32),
             vmem(1024, 512),
@@ -560,8 +561,7 @@
             vmem(4, 1024, 512),
             vmem(2, 1024, 512),
             vmem(2, 512, 512),
-            vmem(4, 128, 256),
-            sems(16),
+            sems(8),
             sems(3, 15), sems(3, 15),
             sems(15), sems(15),
             sems(15), sems(15),
@@ -576,10 +576,18 @@
             sems(6), sems(6),
         ],
         compiler_params=pltpu.CompilerParams(
-            collective_id=0, has_side_effects=True, vmem_limit_bytes=63 << 20
+            collective_id=0, has_side_effects=True, vmem_limit_bytes=58 << 20
         ),
     )(*flat, out_grad, wo)
-    lay, dq, dk, dv, pg = out
+    lay, dq, dk, dv, pg = pl.pallas_call(
+        store,
+        name="store",
+        out_shape=tuple(jax.ShapeDtypeStruct(t.shape, t.dtype) for t in out),
+        in_specs=[any_spec] * 5,
+        out_specs=[any_spec] * 5,
+        scratch_shapes=[sems(5)],
+        compiler_params=pltpu.CompilerParams(vmem_limit_bytes=1 << 20),
+    )(*out)
     return lay, *(t.reshape(1024, 4, 128) for t in (dq, dk, dv)), pg
 
 

time: 122 us -> 112 us (0.918)
  local copies, waits for them, and re-layouts: 10.7 us -> 0 us
    unnamed x7 -> x0, local copies, waits for them, and re-layouts: 10.7 us -> none
    pallas_call x1 -> x2, Pallas kernels: 110 us -> 111 us  [the longest x1 109 us: on_device(): pl.pallas_call(kernel, name='layer', out_shape=(pltpu.VMEM((1024, 512), B...]
where the time goes in v3:
time: 112 us
  Pallas kernels  111 us (99%)
    pallas_call x1, Pallas kernels, on_device(): pl.pallas_call(kernel, name='layer', out_shape=(pltpu.VMEM((1024, 512), B...  109 us

profile of v3, /device:TPU:1, one launch (start us, length us, event | category | flops | bytes accessed | tf_op | source)
XLA Modules:
  0.0 112.1 jit_solution(12319119236376177018)
XLA Ops:
  0.6 109.3 %layer.1 = (bf16[1024,512]{1,0:T(8,128)(2,1)S(1)}, bf16[4096,128]{1,0:T(8,128)(2,1)S(1)}, bf16[4096,128]{1,0:T(8,128)(2,1)S(1)}, bf16[4096,128]{1,0:T(8,128)(2,1)S(1)}, bf16[512,256]{1,0:T(8,128)(2,1)S(1)}) custom-call(bf16[4096,128]{1,0:T(8,128)(2,1)} %bitcast.6, bf16[4096,128]{1,0:T(8,128)(2,1)} %bitcast.7, bf16[4096,128]{1,0:T(8,128)(2,1)} %bitcast.8, ...), custom_call_target="tpu_custom_call" | custom-call | tf_op jit(solution)/shard_map/layer/pallas_call | solution.py:528
  110.0 2.1 %store.1 = (bf16[1024,512]{1,0:T(8,128)(2,1)}, bf16[4096,128]{1,0:T(8,128)(2,1)}, bf16[4096,128]{1,0:T(8,128)(2,1)}, bf16[4096,128]{1,0:T(8,128)(2,1)}, bf16[512,256]{1,0:T(8,128)(2,1)}) custom-call(bf16[1024,512]{1,0:T(8,128)(2,1)S(1)} %get-tuple-element.15.refs_0_, bf16[4096,128]{1,0:T(8,128)(2,1)S(1)} %get-tuple-element.16.refs_1_, ...), custom_call_target="tpu_custom_call" | custom-call | tf_op jit(solution)/shard_map/store/pallas_call | solution.py:582

commit v4 on v3

--- a/solution.py
+++ b/solution.py
@@ -124,10 +124,10 @@
     pl.semaphore_wait(barrier, 19)
 
     w_own = W.at[:, own_cols]
-    wz, wy = [], []
-    for d in range(1, 4):
-        wz.append(push(remote(w_own, w_own, w1_s.at[d - 1], w1_r.at[d - 1], (grid_peer(0, d), h))))
-        wy.append(push(remote(w_own, w_own, w1_s.at[2 + d], w1_r.at[2 + d], (grid_peer(d, 0), h))))
+    wz, wy = {}, {}
+    for k, d in enumerate((1, 3)):
+        wz[d] = push(remote(w_own, w_own, w1_s.at[k], w1_r.at[k], (grid_peer(0, d), h)))
+        wy[d] = push(remote(w_own, w_own, w1_s.at[2 + k], w1_r.at[2 + k], (grid_peer(d, 0), h)))
 
     qkv_in = []
 
@@ -148,33 +148,41 @@
 
     wa = [[None] * 2 for _ in range(3)]
     wb = [[None] * 2 for _ in range(3)]
+    wr = []
+
+    def spread_along(d):
+        block = w_block(0, 256, grid_peer(0, 4 - d))
+        for k, e in enumerate((1, 3)):
+            wa[d - 1][k] = push(remote(block, block, wa_s.at[d - 1, k], wa_r.at[d - 1, k], (grid_peer(e, 0), h)))
+        block = w_block(256, 256, grid_peer(4 - d, 0))
+        for k, e in enumerate((1, 3)):
+            wb[d - 1][k] = push(remote(block, block, wb_s.at[d - 1, k], wb_r.at[d - 1, k], (grid_peer(0, e), h)))
 
     def spread_w():
-        for d in range(1, 4):
-            wz[d - 1].wait_recv()
-            block = w_block(0, 256, grid_peer(0, 4 - d))
-            for k, e in enumerate((1, 3)):
-                wa[d - 1][k] = push(
-                    remote(block, block, wa_s.at[d - 1, k], wa_r.at[d - 1, k], (grid_peer(e, 0), h))
-                )
-            wy[d - 1].wait_recv()
-            block = w_block(256, 256, grid_peer(4 - d, 0))
-            for k, e in enumerate((1, 3)):
-                wb[d - 1][k] = push(
-                    remote(block, block, wb_s.at[d - 1, k], wb_r.at[d - 1, k], (grid_peer(0, e), h))
-                )
+        for d in (1, 3):
+            wz[d].wait_recv()
+            wy[d].wait_recv()
+        for k, (first, dy, dz) in enumerate(((0, 0, 1), (256, 0, 3), (256, 1, 0), (0, 3, 0))):
+            block = w_block(first, 256, grid_peer((4 - dy) % 4, (4 - dz) % 4))
+            wr.append(push(remote(block, block, w1_s.at[4 + k], w1_r.at[4 + k], (grid_peer(dy, dz), h))))
+        spread_along(1)
+        spread_along(3)
+
+    def spread_far():
+        for copy in wr:
+            copy.wait_recv()
+        spread_along(2)
 
     wc = []
 
-    def relay_w():
-        for d in range(1, 4):
-            for k, e in enumerate((1, 3)):
-                wa[d - 1][k].wait_recv()
-                block = w_block(128 * k, 128, grid_peer(4 - e, 4 - d))
-                wc.append(push(remote(block, block, wc_s.at[0, d - 1, k], wc_r.at[0, d - 1, k], (grid_peer(e, 0), h))))
-                wb[d - 1][k].wait_recv()
-                block = w_block(256 + 128 * k, 128, grid_peer(4 - d, 4 - e))
-                wc.append(push(remote(block, block, wc_s.at[1, d - 1, k], wc_r.at[1, d - 1, k], (grid_peer(0, e), h))))
+    def relay_w(d):
+        for k, e in enumerate((1, 3)):
+            wa[d - 1][k].wait_recv()
+            block = w_block(128 * k, 128, grid_peer(4 - e, 4 - d))
+            wc.append(push(remote(block, block, wc_s.at[0, d - 1, k], wc_r.at[0, d - 1, k], (grid_peer(e, 0), h))))
+            wb[d - 1][k].wait_recv()
+            block = w_block(256 + 128 * k, 128, grid_peer(4 - d, 4 - e))
+            wc.append(push(remote(block, block, wc_s.at[1, d - 1, k], wc_r.at[1, d - 1, k], (grid_peer(0, e), h))))
 
     def unpack_rows(m, carry):
         for t in range(3):
@@ -296,13 +304,16 @@
         return carry
 
     lax.fori_loop(0, 8, col_forward, 0, unroll=2)
+    spread_far()
     o_in = []
     for i, (dy, dz) in enumerate(SEVEN):
         to = grid_peer(dy, dz)
         o_in.append(push(remote(SO.at[to], RO.at[c], o_s.at[i], o_r.at[i], (to, h))))
     RO[c] = SO[c]
 
-    relay_w()
+    relay_w(1)
+    relay_w(3)
+    relay_w(2)
     reduce_start(0)
     reduce_start(1)
 
@@ -322,10 +333,52 @@
         return carry
 
     lax.fori_loop(0, 4, place, 0)
-    projection(1)
 
     for copy in wc:
         copy.wait_recv()
+
+    def partial_out(m, head):
+        rows = pl.ds(pl.multiple_of(m * 256, 256), 256)
+        cols = pl.ds(pl.multiple_of(head * 512, 512), 512)
+        return rows, nn(ATT[rows, :], W[:, cols])
+
+    order = (2, 1, 3, 0)
+    lp_in = [None] * 4
+
+    def to_partner(n):
+        head = lax.rem(x + order[n], 4) * 2 + (1 - core)
+
+        def for_partner(m, carry):
+            rows, part = partial_out(m, head)
+            LS[n, rows, :] = part.astype(BF16)
+            return carry
+
+        lax.fori_loop(0, 4, for_partner, 0)
+        lp_in[n] = push(remote(LS.at[n], LR.at[n], lp_s.at[n], lp_r.at[n], partner))
+
+    def to_x(n):
+        head = x_head(order[n])
+        lp_in[n].wait_recv()
+
+        def for_x(m, carry):
+            rows, part = partial_out(m, head)
+            LR[n, rows, :] = (part + LR[n, rows, :].astype(F32)).astype(BF16)
+            return carry
+
+        lax.fori_loop(0, 4, for_x, 0)
+
+    lower, upper = pl.ds(0, 512), pl.ds(512, 512)
+    ahead, behind = (c, x_head(1)), (c, x_head(3))
+
+    def add_passing(n, k, rows):
+        relay[k].wait_recv()
+        LR[n, rows, :] = (LR[n, rows, :].astype(F32) + XR[k].astype(F32)).astype(BF16)
+
+    def add_x():
+        add_passing(1, 0, lower)
+        lx_in.append(push(remote(LR.at[1, lower], LX.at[0, lower], lx_s.at[4], lx_r.at[4], ahead)))
+        add_passing(2, 1, upper)
+        lx_in.append(push(remote(LR.at[2, upper], LX.at[1, upper], lx_s.at[5], lx_r.at[5], behind)))
 
     def strided_cotangent(m, carry):
         rows = pl.ds(pl.multiple_of(m * 256, 256), 256)
@@ -345,47 +398,6 @@
         to = grid_peer(dy, dz)
         do_in.append(push(remote(SO.at[to], RDO.at[c], do_s.at[i], do_r.at[i], (to, h))))
     RDO[c] = SO[c]
-    reduce_start(2)
-    reduce_start(3)
-    reduce_pass(0)
-    reduce_pass(1)
-
-    def partial_out(m, head):
-        rows = pl.ds(pl.multiple_of(m * 256, 256), 256)
-        cols = pl.ds(pl.multiple_of(head * 512, 512), 512)
-        return rows, nn(ATT[rows, :], W[:, cols])
-
-    order = (2, 1, 3, 0)
-    lp_in = [None] * 4
-
-    def to_partner(n):
-        head = lax.rem(x + order[n], 4) * 2 + (1 - core)
-
-        def for_partner(m, carry):
-            rows, part = partial_out(m, head)
-            LS[n, rows, :] = part.astype(BF16)
-            return carry
-
-        lax.fori_loop(0, 4, for_partner, 0)
-        lp_in[n] = push(remote(LS.at[n], LR.at[n], lp_s.at[n], lp_r.at[n], partner))
-
-    def to_x(n):
-        head = x_head(order[n])
-        lp_in[n].wait_recv()
-
-        def for_x(m, carry):
-            rows, part = partial_out(m, head)
-            LR[n, rows, :] = (part + LR[n, rows, :].astype(F32)).astype(BF16)
-            return carry
-
-        lax.fori_loop(0, 4, for_x, 0)
-
-    lower, upper = pl.ds(0, 512), pl.ds(512, 512)
-    ahead, behind = (c, x_head(1)), (c, x_head(3))
-
-    def add_passing(n, k, rows):
-        relay[k].wait_recv()
-        LR[n, rows, :] = (LR[n, rows, :].astype(F32) + XR[k].astype(F32)).astype(BF16)
 
     to_partner(0)
     to_partner(1)
@@ -394,12 +406,21 @@
         push(remote(LR.at[0, lower], XR.at[0], lx_s.at[0], lx_r.at[0], ahead)),
         push(remote(LR.at[0, upper], XR.at[1], lx_s.at[1], lx_r.at[1], behind)),
     ]
+    reduce_pass(0)
+    reduce_pass(1)
+    projection(1)
+    reduce_start(2)
+    reduce_start(3)
+
     to_partner(2)
     to_x(1)
     lx_in = [push(remote(LR.at[1, upper], LX.at[0, upper], lx_s.at[2], lx_r.at[2], ahead))]
     to_partner(3)
     to_x(2)
     lx_in.append(push(remote(LR.at[2, lower], LX.at[1, lower], lx_s.at[3], lx_r.at[3], behind)))
+
+    reduce_middle(0)
+    reduce_middle(1)
 
     for copy in do_in:
         copy.wait_recv()
@@ -426,13 +447,7 @@
         RDG[t, c] = QS[t, c]
 
     to_x(3)
-    add_passing(1, 0, lower)
-    lx_in.append(push(remote(LR.at[1, lower], LX.at[0, lower], lx_s.at[4], lx_r.at[4], ahead)))
-    add_passing(2, 1, upper)
-    lx_in.append(push(remote(LR.at[2, upper], LX.at[1, upper], lx_s.at[5], lx_r.at[5], behind)))
-
-    reduce_middle(0)
-    reduce_middle(1)
+    add_x()
     reduce_middle(2)
     reduce_middle(3)
 
@@ -468,14 +483,11 @@
 
     lax.fori_loop(0, 4, row_backward, 0)
 
-    for q in range(4):
-        reduce_end(q)
-
-    for t in range(3):
+    def join_strided(t):
         for copy in dg_in[15 * t : 15 * t + 15]:
             copy.wait_recv()
 
-        def spread(m, carry, t=t):
+        def spread(m, carry):
             for hh in range(2):
                 block = RDG[t, pl.ds(m * 4, 4), hh].astype(F32)
                 for r in range(2):
@@ -485,14 +497,12 @@
 
         lax.fori_loop(0, 4, spread, 0)
 
-        def narrow(m, carry, t=t):
+        def narrow(m, carry):
             rows = pl.ds(pl.multiple_of(m * 512, 512), 512)
             flat_out[t][rows, :] = WIDE[t, rows, :].astype(BF16)
             return carry
 
         lax.fori_loop(0, 8, narrow, 0)
-    for copy in lx_in:
-        copy.wait_recv()
 
     def finish(m, carry):
         rows = pl.ds(pl.multiple_of(m * 256, 256), 256)
@@ -500,7 +510,16 @@
         lay_out[rows, :] = total.astype(BF16)
         return carry
 
+    reduce_end(0)
+    reduce_end(1)
+    join_strided(0)
+    join_strided(1)
+    for copy in lx_in:
+        copy.wait_recv()
     lax.fori_loop(0, 4, finish, 0)
+    join_strided(2)
+    reduce_end(2)
+    reduce_end(3)
     for copy in sends:
         copy.wait_send()
 
@@ -566,7 +585,7 @@
             sems(15), sems(15),
             sems(15), sems(15),
             sems(3, 15), sems(3, 15),
-            sems(6), sems(6),
+            sems(8), sems(8),
             sems(3, 2), sems(3, 2),
             sems(3, 2), sems(3, 2),
             sems(2, 3, 2), sems(2, 3, 2),

time: 112 us -> 109 us (0.973)
  Pallas kernels: 111 us -> 108 us
    pallas_call x1, Pallas kernels: 109 us -> 106 us  [on_device(): pl.pallas_call(kernel, name='layer', out_shape=(pltpu.VMEM((1024, 512), B...]
where the time goes in v4:
time: 109 us
  Pallas kernels  108 us (99%)
    pallas_call x1, Pallas kernels, on_device(): pl.pallas_call(kernel, name='layer', out_shape=(pltpu.VMEM((1024, 512), B...  106 us

profile of v4, /device:TPU:1, one launch (start us, length us, event | category | flops | bytes accessed | tf_op | source)
XLA Modules:
  0.0 108.7 jit_solution(3985563074704437061)
XLA Ops:
  0.6 105.9 %layer.1 = (bf16[1024,512]{1,0:T(8,128)(2,1)S(1)}, bf16[4096,128]{1,0:T(8,128)(2,1)S(1)}, bf16[4096,128]{1,0:T(8,128)(2,1)S(1)}, bf16[4096,128]{1,0:T(8,128)(2,1)S(1)}, bf16[512,256]{1,0:T(8,128)(2,1)S(1)}) custom-call(bf16[4096,128]{1,0:T(8,128)(2,1)} %bitcast.6, bf16[4096,128]{1,0:T(8,128)(2,1)} %bitcast.7, bf16[4096,128]{1,0:T(8,128)(2,1)} %bitcast.8, ...), custom_call_target="tpu_custom_call" | custom-call | tf_op jit(solution)/shard_map/layer/pallas_call | solution.py:547
  106.6 2.1 %store.1 = (bf16[1024,512]{1,0:T(8,128)(2,1)}, bf16[4096,128]{1,0:T(8,128)(2,1)}, bf16[4096,128]{1,0:T(8,128)(2,1)}, bf16[4096,128]{1,0:T(8,128)(2,1)}, bf16[512,256]{1,0:T(8,128)(2,1)}) custom-call(bf16[1024,512]{1,0:T(8,128)(2,1)S(1)} %get-tuple-element.15.refs_0_, bf16[4096,128]{1,0:T(8,128)(2,1)S(1)} %get-tuple-element.16.refs_1_, ...), custom_call_target="tpu_custom_call" | custom-call | tf_op jit(solution)/shard_map/store/pallas_call | solution.py:601

commit v5 on v4

--- a/solution.py
+++ b/solution.py
@@ -123,23 +123,22 @@
         copy.wait()
     pl.semaphore_wait(barrier, 19)
 
+    qkv_in = []
+
+    def send_strided(t):
+        for i, (dy, dz) in enumerate(SEVEN):
+            to = grid_peer(dy, dz)
+            qkv_in.append(push(remote(QS.at[t, to], REC.at[t, c], qkv_s.at[t, i], qkv_r.at[t, i], (to, h))))
+        REC[t, c] = QS[t, c]
+
+    send_strided(0)
+    unpack(1)
+    send_strided(1)
     w_own = W.at[:, own_cols]
     wz, wy = {}, {}
     for k, d in enumerate((1, 3)):
         wz[d] = push(remote(w_own, w_own, w1_s.at[k], w1_r.at[k], (grid_peer(0, d), h)))
         wy[d] = push(remote(w_own, w_own, w1_s.at[2 + k], w1_r.at[2 + k], (grid_peer(d, 0), h)))
-
-    qkv_in = []
-
-    def send_strided(t):
-        for i, (dy, dz) in enumerate(SEVEN):
-            to = grid_peer(dy, dz)
-            qkv_in.append(push(remote(QS.at[t, to], REC.at[t, c], qkv_s.at[t, i], qkv_r.at[t, i], (to, h))))
-        REC[t, c] = QS[t, c]
-
-    send_strided(0)
-    unpack(1)
-    send_strided(1)
     unpack(2)
     send_strided(2)
 
@@ -225,9 +224,9 @@
 
         lax.fori_loop(0, 16, one, 0)
 
-    spread_w()
     load_og.wait()
     projection(0)
+    spread_w()
 
     first_half, second_half = pl.ds(0, 2), pl.ds(2, 2)
 
@@ -333,6 +332,9 @@
         return carry
 
     lax.fori_loop(0, 4, place, 0)
+    projection(1)
+    reduce_start(2)
+    reduce_start(3)
 
     for copy in wc:
         copy.wait_recv()
@@ -379,6 +381,14 @@
         lx_in.append(push(remote(LR.at[1, lower], LX.at[0, lower], lx_s.at[4], lx_r.at[4], ahead)))
         add_passing(2, 1, upper)
         lx_in.append(push(remote(LR.at[2, upper], LX.at[1, upper], lx_s.at[5], lx_r.at[5], behind)))
+
+    to_partner(0)
+    to_partner(1)
+    to_x(0)
+    relay = [
+        push(remote(LR.at[0, lower], XR.at[0], lx_s.at[0], lx_r.at[0], ahead)),
+        push(remote(LR.at[0, upper], XR.at[1], lx_s.at[1], lx_r.at[1], behind)),
+    ]
 
     def strided_cotangent(m, carry):
         rows = pl.ds(pl.multiple_of(m * 256, 256), 256)
@@ -398,19 +408,8 @@
         to = grid_peer(dy, dz)
         do_in.append(push(remote(SO.at[to], RDO.at[c], do_s.at[i], do_r.at[i], (to, h))))
     RDO[c] = SO[c]
-
-    to_partner(0)
-    to_partner(1)
-    to_x(0)
-    relay = [
-        push(remote(LR.at[0, lower], XR.at[0], lx_s.at[0], lx_r.at[0], ahead)),
-        push(remote(LR.at[0, upper], XR.at[1], lx_s.at[1], lx_r.at[1], behind)),
-    ]
     reduce_pass(0)
     reduce_pass(1)
-    projection(1)
-    reduce_start(2)
-    reduce_start(3)
 
     to_partner(2)
     to_x(1)
@@ -419,6 +418,16 @@
     to_x(2)
     lx_in.append(push(remote(LR.at[2, lower], LX.at[1, lower], lx_s.at[3], lx_r.at[3], behind)))
 
+    reduce_pass(2)
+    reduce_pass(3)
+    to_x(3)
+
+    def row_cotangent(m, carry):
+        rows = pl.ds(pl.multiple_of(m * 256, 256), 256)
+        AGR[rows, :] = nt(OG[rows, :], W[pl.ds(0, 256), :]).astype(BF16)
+        return carry
+
+    lax.fori_loop(0, 4, row_cotangent, 0)
     reduce_middle(0)
     reduce_middle(1)
 
@@ -437,8 +446,6 @@
 
     drain(qkv_in)
     lax.fori_loop(0, 8, col_backward, 0, unroll=2)
-    reduce_pass(2)
-    reduce_pass(3)
     dg_in = []
     for t in range(3):
         for i, (dy, dz) in enumerate(SEVEN):
@@ -446,17 +453,9 @@
             dg_in.append(push(remote(QS.at[t, to], RDG.at[t, c], dg_s.at[t, i], dg_r.at[t, i], (to, h))))
         RDG[t, c] = QS[t, c]
 
-    to_x(3)
     add_x()
     reduce_middle(2)
     reduce_middle(3)
-
-    def row_cotangent(m, carry):
-        rows = pl.ds(pl.multiple_of(m * 256, 256), 256)
-        AGR[rows, :] = nt(OG[rows, :], W[pl.ds(0, 256), :]).astype(BF16)
-        return carry
-
-    lax.fori_loop(0, 4, row_cotangent, 0)
 
     def row_backward(i, carry):
         r, hh = i // 2, lax.rem(i, 2)
@@ -510,14 +509,14 @@
         lay_out[rows, :] = total.astype(BF16)
         return carry
 
-    reduce_end(0)
-    reduce_end(1)
     join_strided(0)
     join_strided(1)
     for copy in lx_in:
         copy.wait_recv()
     lax.fori_loop(0, 4, finish, 0)
     join_strided(2)
+    reduce_end(0)
+    reduce_end(1)
     reduce_end(2)
     reduce_end(3)
     for copy in sends:

time: 109 us -> 108 us (level)
  no operation moved by 1% of the time
where the time goes in v5:
time: 108 us
  Pallas kernels  107 us (99%)
    pallas_call x1, Pallas kernels, on_device(): pl.pallas_call(kernel, name='layer', out_shape=(pltpu.VMEM((1024, 512), B...  105 us

profile of v5, /device:TPU:1, one launch (start us, length us, event | category | flops | bytes accessed | tf_op | source)
XLA Modules:
  0.0 108.0 jit_solution(9360514879204084254)
XLA Ops:
  0.6 105.2 %layer.1 = (bf16[1024,512]{1,0:T(8,128)(2,1)S(1)}, bf16[4096,128]{1,0:T(8,128)(2,1)S(1)}, bf16[4096,128]{1,0:T(8,128)(2,1)S(1)}, bf16[4096,128]{1,0:T(8,128)(2,1)S(1)}, bf16[512,256]{1,0:T(8,128)(2,1)S(1)}) custom-call(bf16[4096,128]{1,0:T(8,128)(2,1)} %bitcast.6, bf16[4096,128]{1,0:T(8,128)(2,1)} %bitcast.7, bf16[4096,128]{1,0:T(8,128)(2,1)} %bitcast.8, ...), custom_call_target="tpu_custom_call" | custom-call | tf_op jit(solution)/shard_map/layer/pallas_call | solution.py:546
  105.9 2.1 %store.1 = (bf16[1024,512]{1,0:T(8,128)(2,1)}, bf16[4096,128]{1,0:T(8,128)(2,1)}, bf16[4096,128]{1,0:T(8,128)(2,1)}, bf16[4096,128]{1,0:T(8,128)(2,1)}, bf16[512,256]{1,0:T(8,128)(2,1)}) custom-call(bf16[1024,512]{1,0:T(8,128)(2,1)S(1)} %get-tuple-element.15.refs_0_, bf16[4096,128]{1,0:T(8,128)(2,1)S(1)} %get-tuple-element.16.refs_1_, ...), custom_call_target="tpu_custom_call" | custom-call | tf_op jit(solution)/shard_map/store/pallas_call | solution.py:600
